TPU v7x, 32 devices: a whole 2x2x4 slice. The times are simulated.
32 devices in a mesh: ctx: 8 (over y, x, core), fsdp: 4 (over z).
Axes of the slice: x: 2, y: 2, z: 4, core: 2. Of those that a mesh axis runs over, the one named last changes fastest.
Arguments:
- inputs: bfloat16 [4, 1024, 2048], P('fsdp', 'ctx'), may hold values from -24 to 24
- block_order: int32 [16], replicated, may hold values from 0 to 15, each once
- norm_gains: bfloat16 [2, 2048], P(None, 'fsdp'), may hold values from 0.099609375 to 1.8984375
- w_query: bfloat16 [2048, 2048], P('fsdp'), may hold values from -0.125 to 0.125
- w_key: bfloat16 [256, 2048], P('fsdp'), may hold values from -0.125 to 0.125
- w_value: bfloat16 [256, 2048], P('fsdp'), may hold values from -0.125 to 0.125
- w_output: bfloat16 [2048, 2048], P('fsdp'), may hold values from -3 to 3
- w_gate: bfloat16 [5632, 2048], P('fsdp'), may hold values from -0.125 to 0.125
- w_up: bfloat16 [5632, 2048], P('fsdp'), may hold values from -0.125 to 0.125
- w_down: bfloat16 [2048, 5632], P('fsdp'), may hold values from -0.078125 to 0.078125
- out_grad: bfloat16 [4, 1024, 2048], P('fsdp', 'ctx'), may hold values from -6 to 6
Outputs:
- layer_out: bfloat16 [4, 1024, 2048], P('fsdp', 'ctx')
- grad_inputs: float32 [4, 1024, 2048], P('fsdp', 'ctx')
- grad_gains: float32 [2, 2048], P(None, 'fsdp')
- grad_query: float32 [2048, 2048], P('fsdp', 'ctx')
- grad_key: float32 [256, 2048], P('fsdp', 'ctx')
- grad_value: float32 [256, 2048], P('fsdp', 'ctx')
- grad_output: float32 [2048, 2048], P('fsdp', 'ctx')
- grad_gate: float32 [5632, 2048], P('fsdp', 'ctx')
- grad_up: float32 [5632, 2048], P('fsdp', 'ctx')
- grad_down: float32 [2048, 5632], P('fsdp', 'ctx')
All inputs are finite; a program needn't handle non-finite values.
Results may differ from a plain program's by a relative error of at most 0.022.
Values may be sent and summed in bfloat16 or wider, within the bound.
No kernel may reach another device: no remote copies, remote signals or barrier semaphores. Data moves between devices by JAX's collectives and lax.ppermute only.
A program may use at most 320 MiB of HBM per device.

v0:
```python
import jax
import jax.numpy as jnp
from jax import lax
from jax.sharding import PartitionSpec as P

HEADS = 32
KV_HEADS = 4
HEAD_DIM = 64
BLOCK = 512


rms_eps = 1e-05
rope_base = 10000.0
masked_score = -1e30


def linear(values, weight):
    return lax.dot_general(
        values, weight, (((1,), (1,)), ((), ())), preferred_element_type=jnp.float32
    )


def weight_grad(gradient, values):
    return lax.dot_general(
        gradient, values, (((0,), (0,)), ((), ())), preferred_element_type=jnp.float32
    )


def back_into(gradient, weight):
    return jnp.dot(gradient, weight, preferred_element_type=jnp.float32)


def rotate(values, cosine, sine_table):
    half_dim = values.shape[-1] // 2
    turned = jnp.concatenate([-values[..., half_dim:], values[..., :half_dim]], axis=-1)
    return values * cosine + turned * sine_table


def rotate_back(values, cosine, sine_table):
    half_dim = values.shape[-1] // 2
    scaled = values * sine_table
    turned = jnp.concatenate([scaled[..., half_dim:], -scaled[..., :half_dim]], axis=-1)
    return values * cosine + turned


def rope_tables(positions):
    frequency = rope_base ** (-jnp.arange(0, HEAD_DIM, 2).astype(jnp.float32) / HEAD_DIM)
    angles = positions.astype(jnp.float32)[:, None] * frequency[None, :]
    cosine = jnp.concatenate([jnp.cos(angles), jnp.cos(angles)], axis=-1)[:, None, :]
    sine_table = jnp.concatenate([jnp.sin(angles), jnp.sin(angles)], axis=-1)[:, None, :]
    return (cosine, sine_table)


def norm_forward(values, gain_row):
    inverse = lax.rsqrt(jnp.mean(values * values, axis=-1, keepdims=True) + rms_eps)
    return (values * inverse * gain_row, inverse)


def norm_backward(gradient, values, inverse, gain_row):
    scaled = gradient * gain_row
    inner_mean = jnp.mean(scaled * values, axis=-1, keepdims=True)
    return (
        inverse * scaled - values * inverse**3 * inner_mean,
        jnp.sum(gradient * values * inverse, axis=0),
    )


def score_block(grouped, key_block, key_pos, query_positions, score_scale):
    raw_scores = jnp.einsum(
        "qgha,kga->ghqk", grouped, key_block, preferred_element_type=jnp.float32
    )
    visible = key_pos[None, :] <= query_positions[:, None]
    return jnp.where(visible, raw_scores * score_scale, masked_score)


def row_totals(grouped, key_blocks, pos_blocks, query_positions, score_scale):
    row_shape = (grouped.shape[1], grouped.shape[2], grouped.shape[0])

    def advance(carried, block_item):
        running_max, running_sum = carried
        key_block, key_pos = block_item
        scores = score_block(grouped, key_block, key_pos, query_positions, score_scale)
        new_max = jnp.maximum(running_max, jnp.max(scores, axis=-1))
        new_sum = running_sum * jnp.exp(running_max - new_max) + jnp.sum(
            jnp.exp(scores - new_max[..., None]), axis=-1
        )
        return ((new_max, new_sum), None)

    starting = (jnp.full(row_shape, masked_score, jnp.float32), jnp.zeros(row_shape, jnp.float32))
    totals, unused = lax.scan(advance, starting, (key_blocks, pos_blocks))
    return totals


def attend_forward(
    grouped, key_blocks, value_blocks, pos_blocks, query_positions, score_scale, row_max, row_sum
):

    def accumulate(running_total, block_item):
        key_block, value_block, key_pos = block_item
        scores = score_block(grouped, key_block, key_pos, query_positions, score_scale)
        attention = (jnp.exp(scores - row_max[..., None]) / row_sum[..., None]).astype(jnp.bfloat16)
        update = jnp.einsum(
            "ghqk,kga->qgha", attention, value_block, preferred_element_type=jnp.float32
        )
        return (running_total + update, None)

    starting = jnp.zeros(grouped.shape, jnp.float32)
    result, unused = lax.scan(accumulate, starting, (key_blocks, value_blocks, pos_blocks))
    return result


def attend_delta(
    grouped,
    d_mixed,
    key_blocks,
    value_blocks,
    pos_blocks,
    query_positions,
    score_scale,
    row_max,
    row_sum,
):

    def accumulate(running_total, block_item):
        key_block, value_block, key_pos = block_item
        scores = score_block(grouped, key_block, key_pos, query_positions, score_scale)
        attention = jnp.exp(scores - row_max[..., None]) / row_sum[..., None]
        d_prob = jnp.einsum(
            "qgha,kga->ghqk", d_mixed, value_block, preferred_element_type=jnp.float32
        )
        return (running_total + jnp.sum(d_prob * attention, axis=-1), None)

    starting = jnp.zeros(row_max.shape, jnp.float32)
    result, unused = lax.scan(accumulate, starting, (key_blocks, value_blocks, pos_blocks))
    return result


def attend_backward(
    grouped,
    d_mixed,
    key_blocks,
    value_blocks,
    pos_blocks,
    query_positions,
    score_scale,
    row_max,
    row_sum,
    row_delta,
):

    def accumulate(d_query, block_item):
        key_block, value_block, key_pos = block_item
        scores = score_block(grouped, key_block, key_pos, query_positions, score_scale)
        attention = jnp.exp(scores - row_max[..., None]) / row_sum[..., None]
        attention_low = attention.astype(jnp.bfloat16)
        d_prob = jnp.einsum(
            "qgha,kga->ghqk", d_mixed, value_block, preferred_element_type=jnp.float32
        )
        d_raw = (attention * (d_prob - row_delta[..., None]) * score_scale).astype(jnp.bfloat16)
        d_query = d_query + jnp.einsum(
            "ghqk,kga->qgha", d_raw, key_block, preferred_element_type=jnp.float32
        )
        d_key_block = jnp.einsum(
            "ghqk,qgha->kga", d_raw, grouped, preferred_element_type=jnp.float32
        )
        d_value_block = jnp.einsum(
            "ghqk,qgha->kga", attention_low, d_mixed, preferred_element_type=jnp.float32
        )
        return (d_query, (d_key_block, d_value_block))

    starting = jnp.zeros(grouped.shape, jnp.float32)
    return lax.scan(accumulate, starting, (key_blocks, value_blocks, pos_blocks))


def per_device(
    inputs,
    block_order,
    norm_gains,
    w_query,
    w_key,
    w_value,
    w_output,
    w_gate,
    w_up,
    w_down,
    out_grad,
):
    ctx_size = lax.axis_size("ctx")
    tokens = inputs.shape[1]
    seqlen = tokens * ctx_size
    half_len = tokens // 2
    groups = HEADS // KV_HEADS
    kv_width = KV_HEADS * HEAD_DIM
    score_scale = HEAD_DIM ** (-0.5)
    block_count = seqlen // BLOCK
    own_rows = inputs[0].astype(jnp.float32)
    local_weights = (norm_gains, w_query, w_key, w_value, w_output, w_gate, w_up, w_down)
    gathered = (
        lax.all_gather(local_weights[0], "fsdp", axis=1, tiled=True),
        lax.all_gather(local_weights[1], "fsdp", axis=0, tiled=True),
        lax.all_gather(local_weights[2], "fsdp", axis=0, tiled=True),
        lax.all_gather(local_weights[3], "fsdp", axis=0, tiled=True),
        lax.all_gather(local_weights[4], "fsdp", axis=0, tiled=True),
        lax.all_gather(local_weights[5], "fsdp", axis=0, tiled=True),
        lax.all_gather(local_weights[6], "fsdp", axis=0, tiled=True),
        lax.all_gather(local_weights[7], "fsdp", axis=0, tiled=True),
    )
    full_gains, full_query, full_key, full_value, full_output, full_gate, full_up, full_down = (
        gathered
    )
    offsets = jnp.arange(half_len, dtype=jnp.int32)
    key_positions = (block_order[:, None] * half_len + offsets[None, :]).reshape(seqlen)
    query_positions = lax.dynamic_slice_in_dim(
        key_positions, lax.axis_index("ctx") * tokens, tokens
    )
    cosine, sine_table = rope_tables(query_positions)
    gain_one = full_gains[0].astype(jnp.float32)
    gain_two = full_gains[1].astype(jnp.float32)
    normed_float, inverse_one = norm_forward(own_rows, gain_one)
    normed_one = normed_float.astype(jnp.bfloat16)
    query_lin = linear(normed_one, full_query).reshape(tokens, HEADS, HEAD_DIM)
    key_lin = linear(normed_one, full_key).reshape(tokens, KV_HEADS, HEAD_DIM)
    queries = rotate(query_lin, cosine, sine_table).astype(jnp.bfloat16)
    own_keys = rotate(key_lin, cosine, sine_table).astype(jnp.bfloat16).reshape(tokens, kv_width)
    own_values = linear(normed_one, full_value).astype(jnp.bfloat16)
    all_keys, all_values = (
        lax.all_gather(own_keys, "ctx", axis=0, tiled=True),
        lax.all_gather(own_values, "ctx", axis=0, tiled=True),
    )
    grouped = queries.reshape(tokens, KV_HEADS, groups, HEAD_DIM)
    key_blocks = all_keys.reshape(block_count, BLOCK, KV_HEADS, HEAD_DIM)
    value_blocks = all_values.reshape(block_count, BLOCK, KV_HEADS, HEAD_DIM)
    pos_blocks = key_positions.reshape(block_count, BLOCK)
    row_max, row_sum = row_totals(grouped, key_blocks, pos_blocks, query_positions, score_scale)
    attended = attend_forward(
        grouped,
        key_blocks,
        value_blocks,
        pos_blocks,
        query_positions,
        score_scale,
        row_max,
        row_sum,
    )
    mixed_low = attended.reshape(tokens, HEADS * HEAD_DIM).astype(jnp.bfloat16)
    hidden = own_rows + linear(mixed_low, full_output)
    normed_float_two, inverse_two = norm_forward(hidden, gain_two)
    normed_two = normed_float_two.astype(jnp.bfloat16)
    gate_lin = linear(normed_two, full_gate)
    up_lin = linear(normed_two, full_up)
    sigmoid_gate = jax.nn.sigmoid(gate_lin)
    inner_low = (gate_lin * sigmoid_gate * up_lin).astype(jnp.bfloat16)
    final_rows = hidden + linear(inner_low, full_down)
    layer_out = final_rows.astype(jnp.bfloat16).reshape(1, tokens, final_rows.shape[1])
    refetch, unused = lax.optimization_barrier((local_weights, final_rows))
    back_weights = (
        lax.all_gather(refetch[0], "fsdp", axis=1, tiled=True),
        lax.all_gather(refetch[1], "fsdp", axis=0, tiled=True),
        lax.all_gather(refetch[2], "fsdp", axis=0, tiled=True),
        lax.all_gather(refetch[3], "fsdp", axis=0, tiled=True),
        lax.all_gather(refetch[4], "fsdp", axis=0, tiled=True),
        lax.all_gather(refetch[5], "fsdp", axis=0, tiled=True),
        lax.all_gather(refetch[6], "fsdp", axis=0, tiled=True),
        lax.all_gather(refetch[7], "fsdp", axis=0, tiled=True),
    )
    back_gains, back_query, back_key, back_value, back_output, back_gate, back_up, back_down = (
        back_weights
    )
    back_one = back_gains[0].astype(jnp.float32)
    back_two = back_gains[1].astype(jnp.float32)
    d_final = out_grad[0]
    d_inner = back_into(d_final, back_down)
    d_gate = (d_inner * up_lin * sigmoid_gate * (1.0 + gate_lin * (1.0 - sigmoid_gate))).astype(
        jnp.bfloat16
    )
    d_up = (d_inner * gate_lin * sigmoid_gate).astype(jnp.bfloat16)
    d_normed_two = back_into(d_gate, back_gate) + back_into(d_up, back_up)
    d_from_two, gain_two_grad = norm_backward(d_normed_two, hidden, inverse_two, back_two)
    d_hidden = d_final.astype(jnp.float32) + d_from_two
    d_branch = d_hidden.astype(jnp.bfloat16)
    d_mixed = (
        back_into(d_branch, back_output)
        .astype(jnp.bfloat16)
        .reshape(tokens, KV_HEADS, groups, HEAD_DIM)
    )
    row_delta = attend_delta(
        grouped,
        d_mixed,
        key_blocks,
        value_blocks,
        pos_blocks,
        query_positions,
        score_scale,
        row_max,
        row_sum,
    )
    d_query_rot, (d_key_blocks, d_value_blocks) = attend_backward(
        grouped,
        d_mixed,
        key_blocks,
        value_blocks,
        pos_blocks,
        query_positions,
        score_scale,
        row_max,
        row_sum,
        row_delta,
    )
    key_share, value_share = (
        lax.psum_scatter(
            d_key_blocks.reshape(seqlen, kv_width).astype(jnp.bfloat16),
            "ctx",
            scatter_dimension=0,
            tiled=True,
        ).astype(jnp.float32),
        lax.psum_scatter(
            d_value_blocks.reshape(seqlen, kv_width).astype(jnp.bfloat16),
            "ctx",
            scatter_dimension=0,
            tiled=True,
        ).astype(jnp.float32),
    )
    d_key = (
        rotate_back(key_share.reshape(tokens, KV_HEADS, HEAD_DIM), cosine, sine_table)
        .reshape(tokens, kv_width)
        .astype(jnp.bfloat16)
    )
    d_value = value_share.astype(jnp.bfloat16)
    d_query = (
        rotate_back(d_query_rot.reshape(tokens, HEADS, HEAD_DIM), cosine, sine_table)
        .reshape(tokens, HEADS * HEAD_DIM)
        .astype(jnp.bfloat16)
    )
    d_normed_one = (
        back_into(d_query, back_query) + back_into(d_key, back_key) + back_into(d_value, back_value)
    )
    d_from_one, gain_one_grad = norm_backward(d_normed_one, own_rows, inverse_one, back_one)
    grad_inputs = (d_hidden + d_from_one).reshape(1, tokens, d_hidden.shape[1])
    gain_totals = lax.psum(jnp.stack([gain_one_grad, gain_two_grad]), ("ctx", "fsdp"))
    gain_width = norm_gains.shape[1]
    grad_gains = lax.dynamic_slice_in_dim(
        gain_totals, lax.axis_index("fsdp") * gain_width, gain_width, 1
    )
    weight_terms = (
        weight_grad(d_query, normed_one),
        weight_grad(d_key, normed_one),
        weight_grad(d_value, normed_one),
        weight_grad(d_branch, mixed_low),
        weight_grad(d_gate, normed_two),
        weight_grad(d_up, normed_two),
        weight_grad(d_final, inner_low),
    )
    column_parts = (
        lax.psum_scatter(
            weight_terms[0].astype(jnp.bfloat16), "ctx", scatter_dimension=1, tiled=True
        ).astype(jnp.float32),
        lax.psum_scatter(
            weight_terms[1].astype(jnp.bfloat16), "ctx", scatter_dimension=1, tiled=True
        ).astype(jnp.float32),
        lax.psum_scatter(
            weight_terms[2].astype(jnp.bfloat16), "ctx", scatter_dimension=1, tiled=True
        ).astype(jnp.float32),
        lax.psum_scatter(
            weight_terms[3].astype(jnp.bfloat16), "ctx", scatter_dimension=1, tiled=True
        ).astype(jnp.float32),
        lax.psum_scatter(
            weight_terms[4].astype(jnp.bfloat16), "ctx", scatter_dimension=1, tiled=True
        ).astype(jnp.float32),
        lax.psum_scatter(
            weight_terms[5].astype(jnp.bfloat16), "ctx", scatter_dimension=1, tiled=True
        ).astype(jnp.float32),
        lax.psum_scatter(
            weight_terms[6].astype(jnp.bfloat16), "ctx", scatter_dimension=1, tiled=True
        ).astype(jnp.float32),
    )
    owned = (
        lax.psum_scatter(
            column_parts[0].astype(jnp.bfloat16), "fsdp", scatter_dimension=0, tiled=True
        ).astype(jnp.float32),
        lax.psum_scatter(
            column_parts[1].astype(jnp.bfloat16), "fsdp", scatter_dimension=0, tiled=True
        ).astype(jnp.float32),
        lax.psum_scatter(
            column_parts[2].astype(jnp.bfloat16), "fsdp", scatter_dimension=0, tiled=True
        ).astype(jnp.float32),
        lax.psum_scatter(
            column_parts[3].astype(jnp.bfloat16), "fsdp", scatter_dimension=0, tiled=True
        ).astype(jnp.float32),
        lax.psum_scatter(
            column_parts[4].astype(jnp.bfloat16), "fsdp", scatter_dimension=0, tiled=True
        ).astype(jnp.float32),
        lax.psum_scatter(
            column_parts[5].astype(jnp.bfloat16), "fsdp", scatter_dimension=0, tiled=True
        ).astype(jnp.float32),
        lax.psum_scatter(
            column_parts[6].astype(jnp.bfloat16), "fsdp", scatter_dimension=0, tiled=True
        ).astype(jnp.float32),
    )
    return (
        layer_out,
        grad_inputs,
        grad_gains,
        owned[0],
        owned[1],
        owned[2],
        owned[3],
        owned[4],
        owned[5],
        owned[6],
    )


def solution(mesh):
    placed = (
        P("fsdp", "ctx", None),
        P(),
        P(None, "fsdp"),
        P("fsdp", None),
        P("fsdp", None),
        P("fsdp", None),
        P("fsdp", None),
        P("fsdp", None),
        P("fsdp", None),
        P("fsdp", None),
        P("fsdp", "ctx", None),
    )
    return jax.shard_map(
        per_device,
        mesh=mesh,
        in_specs=placed,
        out_specs=(
            P("fsdp", "ctx", None),
            P("fsdp", "ctx", None),
            P(None, "fsdp"),
            P("fsdp", "ctx"),
            P("fsdp", "ctx"),
            P("fsdp", "ctx"),
            P("fsdp", "ctx"),
            P("fsdp", "ctx"),
            P("fsdp", "ctx"),
            P("fsdp", "ctx"),
        ),
        check_vma=False,
    )
```

profile of v0, /device:TPU:0, one launch (start us, length us, event | category | flops | bytes accessed | tf_op | source)
XLA Modules:
  0.0 4167.7 jit_solution(11910640683097160102)
XLA Ops:
  12.5 13.8 all_gather.54
  27.4 13.0 all-gather.17.cloned.1.call-done
  42.2 10.0 all_gather.58
  52.6 16.7 all-gather.15.cloned.1.call-done
  71.0 10.0 all_gather.56
  82.1 137.8 %all-gather.19.cloned.1.call-done = bf16[2048,2048]{1,0:T(8,128)(2,1)} async-done(((bf16[512,2048]{1,0:T(8,128)(2,1)}), bf16[2048,2048]{1,0:T(8,128)(2,1)}) %all-gather.19.cloned.1.call-update) | async-done | bytes 8388624 | tf_op jit(solution)/shard_map/all_gather | solution.py:200
  219.9 5.9 fusion.91
  226.2 20.7 while.50
  246.9 9.3 while.51
  257.7 111.5 %all-gather.21.cloned.1.call-done = bf16[2048,2048]{1,0:T(8,128)(2,1)} async-done(((bf16[512,2048]{1,0:T(8,128)(2,1)}), bf16[2048,2048]{1,0:T(8,128)(2,1)}) %all-gather.21.cloned.1.call-update) | async-done | bytes 8388624 | tf_op jit(solution)/shard_map/all_gather | solution.py:203
  369.1 6.4 multiply_reduce_fusion.2
  375.7 384.2 %all-gather.23.cloned.1.call-done = bf16[5632,2048]{1,0:T(8,128)(2,1)} async-done(((bf16[1408,2048]{1,0:T(8,128)(2,1)}), bf16[5632,2048]{1,0:T(8,128)(2,1)}) %all-gather.23.cloned.1.call-update) | async-done | bytes 23068688 | tf_op jit(solution)/shard_map/all_gather | solution.py:204
  759.9 14.4 fusion.110
  774.3 376.4 %all-gather.25.cloned.1.call-done = bf16[5632,2048]{1,0:T(8,128)(2,1)} async-done(((bf16[1408,2048]{1,0:T(8,128)(2,1)}), bf16[5632,2048]{1,0:T(8,128)(2,1)}) %all-gather.25.cloned.1.call-update) | async-done | bytes 23068688 | tf_op jit(solution)/shard_map/all_gather | solution.py:205
  1150.7 15.0 multiply_convert_fusion.2
  1165.7 376.0 %all-gather.27.cloned.1.call-done = bf16[2048,5632]{1,0:T(8,128)(2,1)} async-done(((bf16[512,5632]{1,0:T(8,128)(2,1)}), bf16[2048,5632]{1,0:T(8,128)(2,1)}) %all-gather.27.cloned.1.call-update) | async-done | bytes 23068688 | tf_op jit(solution)/shard_map/all_gather | solution.py:206
  1541.7 12.9 convolution_add_fusion.3
  1556.7 12.3 all_gather.67
  1569.7 374.4 %all-gather.29.cloned.1.call-done = bf16[2048,5632]{1,0:T(8,128)(2,1)} async-done(((bf16[512,5632]{1,0:T(8,128)(2,1)}), bf16[2048,5632]{1,0:T(8,128)(2,1)}) %all-gather.29.cloned.1.call-update) | async-done | bytes 23068688 | tf_op jit(solution)/shard_map/all_gather | solution.py:264
  1944.1 17.4 multiply_convert_fusion
  1961.4 373.6 %all-gather.31.cloned.1.call-done = bf16[5632,2048]{1,0:T(8,128)(2,1)} async-done(((bf16[1408,2048]{1,0:T(8,128)(2,1)}), bf16[5632,2048]{1,0:T(8,128)(2,1)}) %all-gather.31.cloned.1.call-update) | async-done | bytes 23068688 | tf_op jit(solution)/shard_map/all_gather | solution.py:262
  2335.1 13.4 fusion.111
  2348.4 377.5 %all-gather.33.cloned.1.call-done = bf16[5632,2048]{1,0:T(8,128)(2,1)} async-done(((bf16[1408,2048]{1,0:T(8,128)(2,1)}), bf16[5632,2048]{1,0:T(8,128)(2,1)}) %all-gather.33.cloned.1.call-update) | async-done | bytes 23068688 | tf_op jit(solution)/shard_map/all_gather | solution.py:263
  2725.9 13.2 multiply_reduce_fusion
  2740.7 134.7 %all-gather.35.cloned.1.call-done = bf16[2048,2048]{1,0:T(8,128)(2,1)} async-done(((bf16[512,2048]{1,0:T(8,128)(2,1)}), bf16[2048,2048]{1,0:T(8,128)(2,1)}) %all-gather.35.cloned.1.call-update) | async-done | bytes 8388624 | tf_op jit(solution)/shard_map/all_gather | solution.py:261
  2882.3 10.8 while.52
  2893.2 35.0 while.53
  2938.6 27.3 reduce-scatter.49.cloned.1.call-done
  2971.5 32.2 reduce-scatter.51.cloned.1.call-done
  3006.3 11.2 convert_bitcast_fusion
  3026.5 5.8 convolution_convert_fusion.3
  3032.4 12.3 convolution_convert_fusion.1
  3045.0 12.7 convolution_convert_fusion
  3060.6 21.1 reduce-scatter.29.cloned.1.call-done
  3081.8 149.8 %reduce-scatter.45.cloned.1.call-done = bf16[2048,704]{0,1:T(8,128)(2,1)} async-done(((bf16[2048,5632]{0,1:T(8,128)(2,1)}), bf16[2048,704]{0,1:T(8,128)(2,1)}) %reduce-scatter.45.cloned.1.call-update) | async-done | bytes 2883600 | tf_op jit(solution)/shard_map/reduce_scatter | solution.py:372
  3231.7 74.6 %reduce-scatter.33.cloned.1.call-done = bf16[2048,256]{1,0:T(8,128)(2,1)} async-done(((bf16[2048,2048]{1,0:T(8,128)(2,1)}), bf16[2048,256]{1,0:T(8,128)(2,1)}) %reduce-scatter.33.cloned.1.call-update) | async-done | bytes 1048592 | tf_op jit(solution)/shard_map/reduce_scatter | solution.py:363
  3306.3 74.5 %reduce-scatter.21.cloned.1.call-done = bf16[2048,256]{1,0:T(8,128)(2,1)} async-done(((bf16[2048,2048]{1,0:T(8,128)(2,1)}), bf16[2048,256]{1,0:T(8,128)(2,1)}) %reduce-scatter.21.cloned.1.call-update) | async-done | bytes 1048592 | tf_op jit(solution)/shard_map/reduce_scatter | solution.py:354
  3380.9 149.6 %reduce-scatter.37.cloned.1.call-done = bf16[5632,256]{1,0:T(8,128)(2,1)} async-done(((bf16[5632,2048]{1,0:T(8,128)(2,1)}), bf16[5632,256]{1,0:T(8,128)(2,1)}) %reduce-scatter.37.cloned.1.call-update) | async-done | bytes 2883600 | tf_op jit(solution)/shard_map/reduce_scatter | solution.py:366
  3530.6 149.5 %reduce-scatter.41.cloned.1.call-done = bf16[5632,256]{1,0:T(8,128)(2,1)} async-done(((bf16[5632,2048]{1,0:T(8,128)(2,1)}), bf16[5632,256]{1,0:T(8,128)(2,1)}) %reduce-scatter.41.cloned.1.call-update) | async-done | bytes 2883600 | tf_op jit(solution)/shard_map/reduce_scatter | solution.py:369
  3681.5 149.8 %all-gather.37.cloned.1.call-done = bf16[2048,2048]{1,0:T(8,128)(2,1)} async-done(((bf16[512,2048]{1,0:T(8,128)(2,1)}), bf16[2048,2048]{1,0:T(8,128)(2,1)}) %all-gather.37.cloned.1.call-update) | async-done | bytes 8388624 | tf_op jit(solution)/shard_map/all_gather | solution.py:258
  3836.0 23.1 all-gather.39.cloned.1.call-done
  3861.6 26.4 all-gather.41.cloned.1.call-done
  3890.2 40.1 psum.7
  3935.1 50.5 %reduce-scatter.47.cloned.1.call-done = bf16[512,704]{0,1:T(8,128)(2,1)} async-done(((bf16[2048,704]{0,1:T(8,128)(2,1)}), bf16[512,704]{0,1:T(8,128)(2,1)}) %reduce-scatter.47.cloned.1.call-update) | async-done | bytes 720912 | tf_op jit(solution)/shard_map/reduce_scatter | solution.py:395
  3988.0 26.8 reduce-scatter.35.cloned.1.call-done
  4016.6 26.3 reduce-scatter.23.cloned.1.call-done
  4044.7 55.4 %reduce-scatter.39.cloned.1.call-done = bf16[1408,256]{1,0:T(8,128)(2,1)} async-done(((bf16[5632,256]{1,0:T(8,128)(2,1)}), bf16[1408,256]{1,0:T(8,128)(2,1)}) %reduce-scatter.39.cloned.1.call-update) | async-done | bytes 720912 | tf_op jit(solution)/shard_map/reduce_scatter | solution.py:389
  4102.4 55.9 %reduce-scatter.43.cloned.1.call-done = bf16[1408,256]{1,0:T(8,128)(2,1)} async-done(((bf16[5632,256]{1,0:T(8,128)(2,1)}), bf16[1408,256]{1,0:T(8,128)(2,1)}) %reduce-scatter.43.cloned.1.call-update) | async-done | bytes 720912 | tf_op jit(solution)/shard_map/reduce_scatter | solution.py:392
  (260 shorter events, 156.6 us)
Async XLA Ops:
  7.2 33.2 all-gather.17.cloned.1.call-start
  7.9 61.4 %all-gather.15.cloned.1.call-start = ((), (), s32[]{:S(2)}) async-start(), calls=%async_computation.16 | async-start | bytes 1310720 | tf_op jit(solution)/shard_map/all_gather | solution.py:202
  8.7 211.2 %all-gather.19.cloned.1.call-start = ((), (), s32[]{:S(2)}) async-start(), calls=%async_computation.18 | async-start | bytes 10485760 | tf_op jit(solution)/shard_map/all_gather | solution.py:200
  9.4 359.7 %all-gather.21.cloned.1.call-start = ((), (), s32[]{:S(2)}) async-start(), calls=%async_computation.19 | async-start | bytes 10485760 | tf_op jit(solution)/shard_map/all_gather | solution.py:203
  10.0 749.9 %all-gather.23.cloned.1.call-start = ((), (), s32[]{:S(2)}) async-start(), calls=%async_computation.20 | async-start | bytes 28835840 | tf_op jit(solution)/shard_map/all_gather | solution.py:204
  10.6 1140.1 %all-gather.25.cloned.1.call-start = ((), (), s32[]{:S(2)}) async-start(), calls=%async_computation.21 | async-start | bytes 28835840 | tf_op jit(solution)/shard_map/all_gather | solution.py:205
  11.2 1530.5 %all-gather.27.cloned.1.call-start = ((), (), s32[]{:S(2)}) async-start(), calls=%async_computation.22 | async-start | bytes 28835840 | tf_op jit(solution)/shard_map/all_gather | solution.py:206
  11.9 1932.2 %all-gather.29.cloned.1.call-start = ((), (), s32[]{:S(2)}) async-start(), calls=%async_computation.23 | async-start | bytes 28835840 | tf_op jit(solution)/shard_map/all_gather | solution.py:264
  26.6 199.3 %copy-start.17 = (f32[128,64]{0,1:T(8,128)}, f32[128,64]{0,1:T(8,128)S(1)}, u32[]{:S(2)}) copy-start(f32[128,64]{0,1:T(8,128)S(1)} %get-tuple-element.592) | copy-start | bytes 98308
  26.6 199.3 %copy-start.19 = (f32[128,64]{0,1:T(8,128)}, f32[128,64]{0,1:T(8,128)S(1)}, u32[]{:S(2)}) copy-start(f32[128,64]{0,1:T(8,128)S(1)} %get-tuple-element.593) | copy-start | bytes 98308
  27.4 192.5 %copy-start.30 = (f32[128]{0:T(128)}, f32[128]{0:T(128)S(1)}, u32[]{:S(2)}) copy-start(f32[128]{0:T(128)S(1)} %get-tuple-element.583) | copy-start | bytes 1540
  27.4 198.4 %copy-start.26 = (f32[1,2048]{1,0:T(1,128)}, f32[1,2048]{1,0:T(1,128)S(1)}, u32[]{:S(2)}) copy-start(f32[1,2048]{1,0:T(1,128)S(1)} %get-tuple-element.579) | copy-start | bytes 24580
  256.1 113.0 %copy-start.8 = (bf16[2,512,4,64]{1,3,2,0:T(8,128)(2,1)}, bf16[2,512,4,64]{1,3,2,0:T(8,128)(2,1)S(1)}, u32[]{:S(2)}) copy-start(bf16[2,512,4,64]{1,3,2,0:T(8,128)(2,1)S(1)} %get-tuple-element.1042) | copy-start | bytes 1572868
  257.6 516.6 %copy-start.13 = (bf16[128,4,8,64]{0,3,2,1:T(8,128)(2,1)}, bf16[128,4,8,64]{0,3,2,1:T(8,128)(2,1)S(1)}, u32[]{:S(2)}) copy-start(bf16[128,4,8,64]{0,3,2,1:T(8,128)(2,1)S(1)} %convert_element_type.191) | copy-start | bytes 1572868
  375.5 2350.4 %copy-start.7 = (f32[128,2048]{1,0:T(8,128)}, f32[128,2048]{1,0:T(8,128)S(1)}, u32[]{:S(2)}) copy-start(f32[128,2048]{1,0:T(8,128)S(1)} %get-tuple-element.587) | copy-start | bytes 3145732
  375.7 775.0 %copy-start.11 = (bf16[128,2048]{1,0:T(8,128)(2,1)}, bf16[128,2048]{1,0:T(8,128)(2,1)S(1)}, u32[]{:S(2)}) copy-start(bf16[128,2048]{1,0:T(8,128)(2,1)S(1)} %multiply_convert_fusion.3) | copy-start | bytes 1572868
  1554.6 780.5 %all-gather.31.cloned.1.call-start = ((), (), s32[]{:S(2)}) async-start(), calls=%async_computation.24 | async-start | bytes 28835840 | tf_op jit(solution)/shard_map/all_gather | solution.py:262
  1555.3 1170.6 %all-gather.33.cloned.1.call-start = ((), (), s32[]{:S(2)}) async-start(), calls=%async_computation.25 | async-start | bytes 28835840 | tf_op jit(solution)/shard_map/all_gather | solution.py:263
  1555.9 1319.5 %all-gather.35.cloned.1.call-start = ((), (), s32[]{:S(2)}) async-start(), calls=%async_computation.26 | async-start | bytes 10485760 | tf_op jit(solution)/shard_map/all_gather | solution.py:261
  1556.6 1409.3 %reduce-scatter.49.cloned.1.call-start = ((), (), s32[]{:S(2)}) async-start(), calls=%async_computation.44 | async-start | bytes 589824
  2740.7 134.7 %copy-start.5 = (f32[128,2048]{1,0:T(8,128)}, f32[128,2048]{1,0:T(8,128)S(1)}, u32[]{:S(2)}) copy-start(f32[128,2048]{1,0:T(8,128)S(1)} %subtract_add_fusion) | copy-start | bytes 3145732
  2928.2 41.7 %copy-start.27 = (f32[1,2048]{1,0:T(1,128)S(1)}, f32[1,2048]{1,0:T(1,128)}, u32[]{:S(2)}) copy-start(f32[1,2048]{1,0:T(1,128)} %copy-done.26) | copy-start | bytes 24580
  2928.2 41.7 %copy-start.31 = (f32[128]{0:T(128)S(1)}, f32[128]{0:T(128)}, u32[]{:S(2)}) copy-start(f32[128]{0:T(128)} %copy-done.30) | copy-start | bytes 1540
  2928.2 78.2 %copy-start.10 = (bf16[128,5632]{1,0:T(8,128)(2,1)S(1)}, bf16[128,5632]{1,0:T(8,128)(2,1)}, u32[]{:S(2)}) copy-start(bf16[128,5632]{1,0:T(8,128)(2,1)} %get-tuple-element.588) | copy-start | bytes 4325380
  2928.2 78.1 %copy-start.16 = (bf16[1,128,2048]{2,1,0:T(8,128)(2,1)S(1)}, bf16[1,128,2048]{2,1,0:T(8,128)(2,1)}, u32[]{:S(2)}) copy-start(bf16[1,128,2048]{2,1,0:T(8,128)(2,1)} %param.29) | copy-start | bytes 1572868
  2933.4 70.3 %reduce-scatter.51.cloned.1.call-start = ((), (), s32[]{:S(2)}) async-start(), calls=%async_computation.45 | async-start | bytes 589824
  2938.5 121.5 %reduce-scatter.25.cloned.1.call-start = ((), (), s32[]{:S(2)}) async-start(), calls=%async_computation.32 | async-start | bytes 1179648 | tf_op jit(solution)/shard_map/reduce_scatter | solution.py:357
  2971.4 110.3 %reduce-scatter.29.cloned.1.call-start = ((), (), s32[]{:S(2)}) async-start(), calls=%async_computation.34 | async-start | bytes 1179648 | tf_op jit(solution)/shard_map/reduce_scatter | solution.py:360
  3006.1 225.5 %reduce-scatter.45.cloned.1.call-start = ((), (), s32[]{:S(2)}) async-start(), calls=%async_computation.42 | async-start | bytes 25952256 | tf_op jit(solution)/shard_map/reduce_scatter | solution.py:372
  3017.6 288.7 %reduce-scatter.33.cloned.1.call-start = ((), (), s32[]{:S(2)}) async-start(), calls=%async_computation.36 | async-start | bytes 9437184 | tf_op jit(solution)/shard_map/reduce_scatter | solution.py:363
  3024.6 356.3 %reduce-scatter.21.cloned.1.call-start = ((), (), s32[]{:S(2)}) async-start(), calls=%async_computation.30 | async-start | bytes 9437184 | tf_op jit(solution)/shard_map/reduce_scatter | solution.py:354
  3032.3 498.2 %reduce-scatter.37.cloned.1.call-start = ((), (), s32[]{:S(2)}) async-start(), calls=%async_computation.38 | async-start | bytes 25952256 | tf_op jit(solution)/shard_map/reduce_scatter | solution.py:366
  3044.7 635.3 %reduce-scatter.41.cloned.1.call-start = ((), (), s32[]{:S(2)}) async-start(), calls=%async_computation.40 | async-start | bytes 25952256 | tf_op jit(solution)/shard_map/reduce_scatter | solution.py:369
  3057.7 773.6 %all-gather.37.cloned.1.call-start = ((), (), s32[]{:S(2)}) async-start(), calls=%async_computation.27 | async-start | bytes 10485760 | tf_op jit(solution)/shard_map/all_gather | solution.py:258
  3058.5 800.6 %all-gather.39.cloned.1.call-start = ((), (), s32[]{:S(2)}) async-start(), calls=%async_computation.28 | async-start | bytes 1310720 | tf_op jit(solution)/shard_map/all_gather | solution.py:259
  3059.2 828.8 %all-gather.41.cloned.1.call-start = ((), (), s32[]{:S(2)}) async-start(), calls=%async_computation.29 | async-start | bytes 1310720 | tf_op jit(solution)/shard_map/all_gather | solution.py:260
  3060.0 872.4 %reduce-scatter.27.cloned.1.call-start = ((), (), s32[]{:S(2)}) async-start(), calls=%async_computation.33 | async-start | bytes 163840 | tf_op jit(solution)/shard_map/reduce_scatter | solution.py:380
  3060.5 873.2 %reduce-scatter.31.cloned.1.call-start = ((), (), s32[]{:S(2)}) async-start(), calls=%async_computation.35 | async-start | bytes 163840 | tf_op jit(solution)/shard_map/reduce_scatter | solution.py:383
  3081.8 903.8 %reduce-scatter.47.cloned.1.call-start = ((), (), s32[]{:S(2)}) async-start(), calls=%async_computation.43 | async-start | bytes 3604480 | tf_op jit(solution)/shard_map/reduce_scatter | solution.py:395
  3231.6 783.2 %reduce-scatter.35.cloned.1.call-start = ((), (), s32[]{:S(2)}) async-start(), calls=%async_computation.37 | async-start | bytes 1310720 | tf_op jit(solution)/shard_map/reduce_scatter | solution.py:386
  3306.3 736.6 %reduce-scatter.23.cloned.1.call-start = ((), (), s32[]{:S(2)}) async-start(), calls=%async_computation.31 | async-start | bytes 1310720 | tf_op jit(solution)/shard_map/reduce_scatter | solution.py:377
  3380.9 719.2 %reduce-scatter.39.cloned.1.call-start = ((), (), s32[]{:S(2)}) async-start(), calls=%async_computation.39 | async-start | bytes 3604480 | tf_op jit(solution)/shard_map/reduce_scatter | solution.py:389
  3530.6 627.8 %reduce-scatter.43.cloned.1.call-start = ((), (), s32[]{:S(2)}) async-start(), calls=%async_computation.41 | async-start | bytes 3604480 | tf_op jit(solution)/shard_map/reduce_scatter | solution.py:392
  3681.5 177.6 %copy-start.22 = (bf16[128,256]{0,1:T(8,128)(2,1)S(1)}, bf16[128,256]{0,1:T(8,128)(2,1)}, u32[]{:S(2)}) copy-start(bf16[128,256]{0,1:T(8,128)(2,1)} %copy-done.21) | copy-start | bytes 196612
  3681.5 206.6 %copy-start.25 = (bf16[128,256]{1,0:T(8,128)(2,1)S(1)}, bf16[128,256]{1,0:T(8,128)(2,1)}, u32[]{:S(2)}) copy-start(bf16[128,256]{1,0:T(8,128)(2,1)} %reduce-scatter.51.cloned.1.call-done) | copy-start | bytes 196612
  3681.5 206.6 %copy-start.28 = (f32[1,2048]{1,0:T(1,128)S(1)}, f32[1,2048]{1,0:T(1,128)}, u32[]{:S(2)}) copy-start(f32[1,2048]{1,0:T(1,128)} %get-tuple-element.576) | copy-start | bytes 24580
  3681.5 208.6 %copy-start.29 = (f32[2048]{0:T(1024)S(1)}, f32[2048]{0:T(1024)}, u32[]{:S(2)}) copy-start(f32[2048]{0:T(1024)} %get-tuple-element.478) | copy-start | bytes 24580
  3681.5 249.4 %copy-start.33 = (f32[128]{0:T(128)S(1)}, f32[128]{0:T(128)}, u32[]{:S(2)}) copy-start(f32[128]{0:T(128)} %get-tuple-element.582) | copy-start | bytes 1540
  (23 other events, 143.7 us)
Sparse Core Ops, SparseCore 0:
  9.6 30.7 all-gather.16
  41.9 27.3 all-gather.14
  70.9 148.9 all-gather.18
  221.3 147.7 all-gather.20
  370.6 389.2 all-gather.22
  761.3 389.3 all-gather.24
  1152.3 389.3 all-gather.26
  1554.7 389.3 all-gather.28
  1945.7 389.3 all-gather.30
  2336.5 389.3 all-gather.32
  2727.5 147.8 all-gather.34
  2933.5 32.3 reduce-scatter.48
  2969.5 34.1 reduce-scatter.50
  3006.7 35.9 reduce-scatter.24
  3045.7 35.9 reduce-scatter.28
  3085.2 146.3 reduce-scatter.44
  3234.9 71.2 reduce-scatter.32
  3309.6 71.2 reduce-scatter.20
  3384.5 146.0 reduce-scatter.36
  3534.0 146.0 reduce-scatter.40
  3681.7 149.5 all-gather.36
  3832.9 26.1 all-gather.38
  3860.7 27.3 all-gather.40
  3890.1 18.8 reduce-scatter.26
  3911.2 17.5 reduce-scatter.30
  3931.0 54.5 reduce-scatter.46
  3987.7 27.0 reduce-scatter.34
  4017.1 25.7 reduce-scatter.22
  4045.2 54.8 reduce-scatter.38
  4102.2 56.0 reduce-scatter.42
where the time goes:
time: 4170 us
  waiting for transfers between devices  3780 us (91%)
  matrix products  222 us (5%)
  blocking collectives  86.3 us (2%)
    all_gather x1, waiting for transfers between devices, per_device(): lax.all_gather(local_weights[5], 'fsdp', axis=0, tiled=True)  384 us
    all_gather x1, waiting for transfers between devices, per_device(): lax.all_gather(refetch[6], 'fsdp', axis=0, tiled=True)  377 us
    all_gather x1, waiting for transfers between devices, per_device(): lax.all_gather(local_weights[6], 'fsdp', axis=0, tiled=True)  376 us
    all_gather x1, waiting for transfers between devices, per_device(): lax.all_gather(local_weights[7], 'fsdp', axis=0, tiled=True)  376 us
    all_gather x1, waiting for transfers between devices, per_device(): lax.all_gather(refetch[7], 'fsdp', axis=0, tiled=True)  374 us
    all_gather x1, waiting for transfers between devices, per_device(): lax.all_gather(refetch[5], 'fsdp', axis=0, tiled=True)  374 us
    reduce_scatter x1, waiting for transfers between devices, per_device(): lax.psum_scatter(weight_terms[6].astype(jnp.bfloat16), 'ctx', scatter_dim...  150 us
    all_gather x1, waiting for transfers between devices, per_device(): lax.all_gather(refetch[1], 'fsdp', axis=0, tiled=True)  150 us
  transfers between devices with their start and end apart: 30, of which 27 were waited for; matrix products, arithmetic and copies ran while one was open for 5% of the time, Pallas kernels for 0%

commit v1 on v0

v1 whole, which is shorter than its diff:
```python
import jax
import jax.numpy as jnp
from jax import lax
from jax.experimental import pallas as pl
from jax.experimental.pallas import tpu as pltpu
from jax.sharding import PartitionSpec as P

HEADS = 32
KV_HEADS = 4
HEAD_DIM = 64
HALF_DIM = HEAD_DIM // 2

rms_eps = 1e-05
rope_base = 10000.0
masked_score = -1e30
score_scale = HEAD_DIM ** (-0.5)

f32 = jnp.float32
bf16 = jnp.bfloat16


def dot(a, b, ca, cb):
    return lax.dot_general(a, b, (((ca,), (cb,)), ((), ())), preferred_element_type=f32)


def unpack_keys(kv_ref, kn, vn, kt, vt):
    blocks, _, tokens = kv_ref.shape
    for b in range(blocks):
        span = slice(b * tokens, (b + 1) * tokens)
        both = kv_ref[b]
        kt[:, span] = both[:HEAD_DIM]
        vt[:, span] = both[HEAD_DIM:]
        turned = both.T
        kn[span, :] = turned[:, :HEAD_DIM]
        vn[span, :] = turned[:, HEAD_DIM:]


def attend_forward_body(q_ref, kv_ref, bias_ref, o_ref, kn, vn, kt, vt):
    unpack_keys(kv_ref, kn, vn, kt, vt)
    heads = q_ref.shape[0] // HEAD_DIM
    bias = jnp.concatenate([bias_ref[...], bias_ref[...]], axis=1)
    tokens = q_ref.shape[1]
    for h in range(0, heads, 2):
        rows = [slice((h + i) * HEAD_DIM, (h + i + 1) * HEAD_DIM) for i in range(2)]
        q2 = jnp.concatenate([q_ref[r, :] for r in rows], axis=1)
        s = dot(kn[...], q2, 1, 0) + bias
        e = jnp.exp(s - jnp.max(s, axis=0, keepdims=True))
        inv = 1.0 / jnp.sum(e, axis=0, keepdims=True)
        o = dot(vt[...], (e * inv).astype(bf16), 1, 0)
        for i in range(2):
            o_ref[rows[i], :] = o[:, i * tokens : (i + 1) * tokens].astype(bf16)


def attend_backward_body(
    q_ref, kv_ref, bias_ref, do_ref, cos_ref, sin_ref, dq_ref, dkv_ref, kn, vn, kt, vt, dk, dv
):
    unpack_keys(kv_ref, kn, vn, kt, vt)
    heads = q_ref.shape[0] // HEAD_DIM
    bias = jnp.concatenate([bias_ref[...], bias_ref[...]], axis=1)
    tokens = q_ref.shape[1]
    cosine, sine = cos_ref[...], sin_ref[...]
    for h in range(0, heads, 2):
        rows = [slice((h + i) * HEAD_DIM, (h + i + 1) * HEAD_DIM) for i in range(2)]
        q2 = jnp.concatenate([q_ref[r, :] for r in rows], axis=1)
        do2 = jnp.concatenate([do_ref[r, :] for r in rows], axis=1)
        q_flat = jnp.concatenate([q_ref[r, :].T for r in rows], axis=0)
        do_flat = jnp.concatenate([do_ref[r, :].T for r in rows], axis=0)
        s = dot(kn[...], q2, 1, 0) + bias
        e = jnp.exp(s - jnp.max(s, axis=0, keepdims=True))
        p = e * (1.0 / jnp.sum(e, axis=0, keepdims=True))
        dp = dot(vn[...], do2, 1, 0)
        delta = jnp.sum(dp * p, axis=0, keepdims=True)
        ds = (p * (dp - delta)).astype(bf16)
        dv_part = dot(p.astype(bf16), do_flat, 1, 0)
        dk_part = dot(ds, q_flat, 1, 0)
        if h == 0:
            dk[...] = dk_part
            dv[...] = dv_part
        else:
            dk[...] += dk_part
            dv[...] += dv_part
        dq2 = dot(kt[...], ds, 1, 0) * score_scale
        for i in range(2):
            dq = dq2[:, i * tokens : (i + 1) * tokens]
            top, low = dq[:HALF_DIM], dq[HALF_DIM:]
            start = (h + i) * HEAD_DIM
            dq_ref[start : start + HALF_DIM, :] = (top * cosine + low * sine).astype(bf16)
            dq_ref[start + HALF_DIM : start + HEAD_DIM, :] = (low * cosine - top * sine).astype(bf16)
    blocks = kv_ref.shape[0]
    for b in range(blocks):
        span = slice(b * tokens, (b + 1) * tokens)
        dkv_ref[b, :HEAD_DIM, :] = dk[span, :].T.astype(bf16)
        dkv_ref[b, HEAD_DIM:, :] = dv[span, :].T.astype(bf16)


def key_scratch(keys):
    return [
        pltpu.VMEM((keys, HEAD_DIM), bf16),
        pltpu.VMEM((keys, HEAD_DIM), bf16),
        pltpu.VMEM((HEAD_DIM, keys), bf16),
        pltpu.VMEM((HEAD_DIM, keys), bf16),
    ]


def attend_forward(q, kv, bias):
    blocks, both, _ = kv.shape
    keys, tokens = bias.shape
    rows, columns = q.shape
    pieces = columns // tokens
    across = pl.BlockSpec((rows, tokens), lambda g: (0, g))
    elements = pieces * (rows // HEAD_DIM) * tokens * keys
    return pl.pallas_call(
        attend_forward_body,
        out_shape=jax.ShapeDtypeStruct(q.shape, bf16),
        grid=(pieces,),
        in_specs=[
            across,
            pl.BlockSpec((blocks, both, tokens), lambda g: (0, 0, g)),
            pl.BlockSpec((keys, tokens), lambda g: (0, 0)),
        ],
        out_specs=across,
        scratch_shapes=key_scratch(keys),
        cost_estimate=pl.CostEstimate(
            flops=4 * elements * HEAD_DIM,
            bytes_accessed=4 * q.size + 2 * kv.size,
            transcendentals=elements,
        ),
        name="attend_forward",
    )(q, kv, bias)


def attend_backward(q, kv, bias, d_out, cosine, sine):
    blocks, both, _ = kv.shape
    keys, tokens = bias.shape
    rows, columns = q.shape
    pieces = columns // tokens
    across = pl.BlockSpec((rows, tokens), lambda g: (0, g))
    whole = pl.BlockSpec((blocks, both, tokens), lambda g: (0, 0, g))
    table = pl.BlockSpec((HALF_DIM, tokens), lambda g: (0, 0))
    elements = pieces * (rows // HEAD_DIM) * tokens * keys
    return pl.pallas_call(
        attend_backward_body,
        out_shape=(jax.ShapeDtypeStruct(q.shape, bf16), jax.ShapeDtypeStruct(kv.shape, bf16)),
        grid=(pieces,),
        in_specs=[
            across,
            whole,
            pl.BlockSpec((keys, tokens), lambda g: (0, 0)),
            across,
            table,
            table,
        ],
        out_specs=(across, whole),
        scratch_shapes=key_scratch(keys)
        + [pltpu.VMEM((keys, HEAD_DIM), f32), pltpu.VMEM((keys, HEAD_DIM), f32)],
        cost_estimate=pl.CostEstimate(
            flops=10 * elements * HEAD_DIM,
            bytes_accessed=6 * q.size + 4 * kv.size,
            transcendentals=elements,
        ),
        name="attend_backward",
    )(q, kv, bias, d_out, cosine, sine)


def fetch(value, k, size):
    if k == 0:
        return value
    return lax.ppermute(value, "fsdp", [((i + k) % size, i) for i in range(size)])


def give(value, k, size):
    if k == 0:
        return value
    return lax.ppermute(value, "fsdp", [(i, (i + k) % size) for i in range(size)])


def spread_columns(weight, ctx_size, fsdp_size):
    rows, columns = weight.shape
    share, width = rows // ctx_size, columns // fsdp_size
    part = lax.dynamic_slice_in_dim(weight, lax.axis_index("ctx") * share, share)
    part = part.reshape(share, fsdp_size, width)
    part = lax.all_to_all(part, "fsdp", split_axis=1, concat_axis=0, tiled=True)
    part = part.reshape(fsdp_size, share, width)
    return lax.all_gather(part, "ctx", axis=1, tiled=True).reshape(rows * fsdp_size, width)


def return_columns(grad, ctx_size, fsdp_size):
    rows, width = grad.shape
    share = rows // (ctx_size * fsdp_size)
    part = grad.reshape(fsdp_size, ctx_size * share, width)
    part = lax.psum_scatter(part, "ctx", scatter_dimension=1, tiled=True)
    part = lax.all_to_all(part, "fsdp", split_axis=0, concat_axis=2, tiled=True)
    part = part.reshape(share, width * fsdp_size)
    return lax.all_to_all(part, "ctx", split_axis=1, concat_axis=0, tiled=True)


def joined(parts, axis=0):
    return parts[0] if len(parts) == 1 else jnp.concatenate(parts, axis=axis)


def inverse_norm(values):
    return lax.rsqrt(jnp.mean(values * values, axis=-1, keepdims=True) + rms_eps)


def per_device(
    inputs,
    block_order,
    norm_gains,
    w_query,
    w_key,
    w_value,
    w_output,
    w_gate,
    w_up,
    w_down,
    out_grad,
):
    C = lax.axis_size("ctx")
    F = lax.axis_size("fsdp")
    z = lax.axis_index("fsdp")
    c = lax.axis_index("ctx")
    tokens, width = inputs.shape[1:]
    keys = tokens * C
    own_x, own_dy = inputs[0], out_grad[0]
    sharing = max(1, F // KV_HEADS)
    kv_rows = w_key.shape[0]
    q_rows = w_query.shape[0]

    x_pieces = [fetch(own_x, k, F) for k in range(F)]
    gains = lax.all_gather(norm_gains, "fsdp", axis=1, tiled=True)
    dy_pieces = [fetch(own_dy, k, F) for k in range(F)]
    w_out = spread_columns(w_output, C, F)
    w_dn = spread_columns(w_down, C, F)

    half_len = keys // block_order.shape[0]
    offsets = jnp.arange(half_len, dtype=jnp.int32)
    key_pos = (block_order[:, None] * half_len + offsets[None, :]).reshape(keys)
    query_pos = lax.dynamic_slice_in_dim(key_pos, c * tokens, tokens)
    bias = jnp.where(key_pos[:, None] <= query_pos[None, :], 0.0, masked_score).astype(f32)
    frequency = rope_base ** (-jnp.arange(0, HEAD_DIM, 2).astype(f32) / HEAD_DIM)
    angles = frequency[:, None] * query_pos.astype(f32)[None, :]
    cosine, sine = jnp.cos(angles), jnp.sin(angles)
    gain_one, gain_two = gains[0].astype(f32), gains[1].astype(f32)

    if sharing > 1:
        groups = [[g * sharing + i for i in range(sharing)] for g in range(F // sharing)]
        both = jnp.stack([w_key, w_value])
        both = lax.all_gather(both, "fsdp", axis=1, tiled=True, axis_index_groups=groups)
        wk, wv = both[0], both[1]
    else:
        wk, wv = w_key, w_value
    w_qkv = jnp.concatenate([w_query, wk, wv], axis=0)

    x_all = joined(x_pieces).astype(f32)
    inv_all = inverse_norm(x_all)
    n1 = (x_all * inv_all * gain_one).astype(bf16)
    lin = dot(w_qkv, n1, 1, 1)

    def rope(values):
        v = values.reshape(-1, 2, HALF_DIM, F, tokens)
        cb, sb = cosine[:, None, :], sine[:, None, :]
        top, low = v[:, 0], v[:, 1]
        out = jnp.stack([top * cb - low * sb, low * cb + top * sb], axis=1)
        return out.reshape(values.shape)

    def rope_back(values):
        v = values.reshape(-1, 2, HALF_DIM, F, tokens)
        cb, sb = cosine[:, None, :], sine[:, None, :]
        top, low = v[:, 0], v[:, 1]
        out = jnp.stack([top * cb + low * sb, low * cb - top * sb], axis=1)
        return out.reshape(values.shape)

    q = (rope(lin[:q_rows]).astype(bf16)) * jnp.asarray(score_scale, bf16)
    kv_own = jnp.concatenate(
        [rope(lin[q_rows : q_rows + HEAD_DIM]).astype(bf16), lin[q_rows + HEAD_DIM :].astype(bf16)]
    )
    kv = lax.all_gather(kv_own, "ctx", axis=0)
    mixed = attend_forward(q, kv, bias)
    part = dot(mixed, w_out, 0, 1)
    hidden = own_x.astype(f32)
    for k in range(F):
        piece = part[k * tokens : (k + 1) * tokens]
        hidden = hidden + (piece if k == 0 else give(piece.astype(bf16), k, F).astype(f32))
    inv_two = inverse_norm(hidden)
    hat_two = hidden * inv_two
    own_n2 = (hat_two * gain_two).astype(bf16)

    n2 = joined([fetch(own_n2, k, F) for k in range(F)])
    dy = joined(dy_pieces)
    gate = dot(n2, w_gate, 1, 1)
    up = dot(n2, w_up, 1, 1)
    d_inner = dot(dy, w_dn, 1, 0)
    sig = jax.nn.sigmoid(gate)
    act = gate * sig
    inner = (act * up).astype(bf16)
    d_gate = (d_inner * up * sig * (1.0 + gate * (1.0 - sig))).astype(bf16)
    d_up = (d_inner * act).astype(bf16)
    dn2_part = dot(d_gate, w_gate, 1, 0) + dot(d_up, w_up, 1, 0)
    d_n2 = jnp.zeros((tokens, width), f32)
    for k in range(F):
        piece = dn2_part[k * tokens : (k + 1) * tokens]
        d_n2 = d_n2 + (piece if k == 0 else give(piece.astype(bf16), k, F).astype(f32))
    out_part = dot(inner, w_dn, 1, 1)
    layer = hidden
    for k in range(F):
        piece = out_part[k * tokens : (k + 1) * tokens]
        layer = layer + (piece if k == 0 else give(piece.astype(bf16), k, F).astype(f32))
    layer_out = layer.astype(bf16).reshape(1, tokens, width)

    scaled = d_n2 * gain_two
    inner_mean = jnp.mean(scaled * hidden, axis=-1, keepdims=True)
    d_hidden = own_dy.astype(f32) + inv_two * scaled - hidden * inv_two**3 * inner_mean
    gain_two_grad = jnp.sum(d_n2 * hat_two, axis=0)
    own_branch = d_hidden.astype(bf16)
    branch = joined([fetch(own_branch, k, F) for k in range(F)])

    d_mixed = dot(w_out, branch, 0, 1).astype(bf16)
    d_q, d_kv = attend_backward(q, kv, bias, d_mixed, cosine, sine)
    d_kv = lax.psum_scatter(d_kv, "ctx", scatter_dimension=0, tiled=False).astype(f32)
    if sharing > 1:
        d_kv = lax.psum(d_kv, "fsdp", axis_index_groups=groups)
    d_k = rope_back(d_kv[:HEAD_DIM]).astype(bf16)
    d_v = d_kv[HEAD_DIM:].astype(bf16)
    if sharing > 1:
        first = (z % sharing) * kv_rows
        d_k = lax.dynamic_slice_in_dim(d_k, first, kv_rows)
        d_v = lax.dynamic_slice_in_dim(d_v, first, kv_rows)
        w_own = jnp.concatenate([w_query, w_key, w_value], axis=0)
    else:
        w_own = w_qkv
    d_qkv = jnp.concatenate([d_q, d_k, d_v], axis=0)
    dn1_part = dot(d_qkv, w_own, 0, 0)
    d_n1 = jnp.zeros((tokens, width), f32)
    for k in range(F):
        piece = dn1_part[k * tokens : (k + 1) * tokens]
        d_n1 = d_n1 + (piece if k == 0 else give(piece.astype(bf16), k, F).astype(f32))
    rows = own_x.astype(f32)
    inv_one = inverse_norm(rows)
    scaled = d_n1 * gain_one
    inner_mean = jnp.mean(scaled * rows, axis=-1, keepdims=True)
    grad_inputs = d_hidden + inv_one * scaled - rows * inv_one**3 * inner_mean
    gain_one_grad = jnp.sum(d_n1 * rows * inv_one, axis=0)
    grad_inputs = grad_inputs.reshape(1, tokens, width)
    gain_totals = lax.psum(jnp.stack([gain_one_grad, gain_two_grad]), ("ctx", "fsdp"))
    gain_width = norm_gains.shape[1]
    grad_gains = lax.dynamic_slice_in_dim(gain_totals, z * gain_width, gain_width, 1)

    def reduced(value):
        return lax.psum_scatter(value.astype(bf16), "ctx", scatter_dimension=1, tiled=True).astype(f32)

    grad_gate = reduced(dot(d_gate, n2, 0, 0))
    grad_up = reduced(dot(d_up, n2, 0, 0))
    grad_down = return_columns(dot(dy, inner, 0, 0).astype(bf16), C, F).astype(f32)
    grad_out = return_columns(dot(branch, mixed, 0, 1).astype(bf16), C, F).astype(f32)
    g_qkv = reduced(dot(d_qkv, n1, 1, 0))
    grad_query = g_qkv[:q_rows]
    grad_key = g_qkv[q_rows : q_rows + kv_rows]
    grad_value = g_qkv[q_rows + kv_rows :]
    return (
        layer_out,
        grad_inputs,
        grad_gains,
        grad_query,
        grad_key,
        grad_value,
        grad_out,
        grad_gate,
        grad_up,
        grad_down,
    )


def solution(mesh):
    rows = P("fsdp", None)
    tokens = P("fsdp", "ctx", None)
    grads = P("fsdp", "ctx")
    return jax.shard_map(
        per_device,
        mesh=mesh,
        in_specs=(tokens, P(), P(None, "fsdp"), rows, rows, rows, rows, rows, rows, rows, tokens),
        out_specs=(tokens, tokens, P(None, "fsdp")) + (grads,) * 7,
        check_vma=False,
    )
```

time: 4170 us -> 809 us (0.19)
  waiting for transfers between devices: 3780 us -> 335 us
  matrix products: 222 us -> 69 us
  starting transfers between devices: 1.64 us -> 142 us
    all_gather x14 -> x3, waiting for transfers between devices: 2880 us -> 1.83 us  [the longest x2 1.83 us: spread_columns(): lax.all_gather(part, 'ctx', axis=1, tiled=True)]
    reduce_scatter x14 -> x4, waiting for transfers between devices: 834 us -> 42 us  [the longest x3 26.9 us: reduced(): lax.psum_scatter(value.astype(bf16), 'ctx', scatter_dimension=1, tiled=True)]
    ppermute x0 -> x24, waiting for transfers between devices: none -> 164 us  [the longest x12 90.4 us: fetch(): lax.ppermute(value, 'fsdp', [((i + k) % size, i) for i in range(size)])]
    dot_general x39 -> x15, matrix products: 222 us -> 69 us  [dot(): lax.dot_general(a, b, (((ca,), (cb,)), ((), ())), preferred_element_type=...]
    ppermute x0 -> x24, starting transfers between devices: none -> 126 us  [the longest x12 65.9 us: fetch(): lax.ppermute(value, 'fsdp', [((i + k) % size, i) for i in range(size)])]
    unnamed x32 -> x9, waiting for transfers between devices: 68.6 us -> 96.6 us
  transfers between devices with their start and end apart: 30 -> 36, of which waited for: 27 -> 17; matrix products, arithmetic and copies ran while one was open for 5% -> 13% of each run, Pallas kernels for 0% -> 2%
where the time goes in v1:
time: 809 us; the launch traced here: 799 us
  waiting for transfers between devices  335 us (41%)
  starting transfers between devices  142 us (18%)
  blocking collectives  127 us (16%)
  matrix products  69 us (9%)
  local copies, waits for them, and re-layouts  50.4 us (6%)
  Pallas kernels  38.8 us (5%)
  other arithmetic  20.4 us (3%)
  between operations  15.9 us (2%)
    unnamed x9, waiting for transfers between devices  96.6 us
    ppermute x12, waiting for transfers between devices, fetch(): lax.ppermute(value, 'fsdp', [((i + k) % size, i) for i in range(size)])  90.4 us
    ppermute x12, waiting for transfers between devices, give(): lax.ppermute(value, 'fsdp', [(i, (i + k) % size) for i in range(size)])  73.7 us
    dot_general x15, matrix products, dot(): lax.dot_general(a, b, (((ca,), (cb,)), ((), ())), preferred_element_type=...  69 us
    ppermute x12, starting transfers between devices, fetch(): lax.ppermute(value, 'fsdp', [((i + k) % size, i) for i in range(size)])  65.9 us
    ppermute x12, starting transfers between devices, give(): lax.ppermute(value, 'fsdp', [(i, (i + k) % size) for i in range(size)])  59.7 us
    psum x1, blocking collectives, per_device(): lax.psum(jnp.stack([gain_one_grad, gain_two_grad]), ('ctx', 'fsdp'))  54 us
    all_gather x1, blocking collectives, per_device(): gains = lax.all_gather(norm_gains, 'fsdp', axis=1, tiled=True)  45.7 us
  transfers between devices with their start and end apart: 36, of which 17 were waited for; matrix products, arithmetic and copies ran while one was open for 13% of the time, Pallas kernels for 2%

profile of v1, /device:TPU:0, one launch (start us, length us, event | category | flops | bytes accessed | tf_op | source)
XLA Modules:
  0.0 799.2 jit_solution(1444131509311602386)
XLA Ops:
  7.3 5.1 collective-permute-start
  13.4 3.1 constant_dynamic-update-slice_fusion.2
  19.4 45.7 %all_gather.15 = bf16[2,2048]{1,0:T(2,128)(2,1)S(1)} all-gather(bf16[2,512]{1,0:T(2,128)(2,1)S(1)} %copy-done.27), channel_id=1, replica_groups=mesh['ctx'=8,'fsdp'=4] {'fsdp'}, dimensions={1}, use_global_device_ids=true | all-gather | bytes 10240 | tf_op jit(solution)/shard_map/all_gather | solution.py:230
  67.0 4.9 fusion.23
  74.0 9.5 %all_to_all.86 = bf16[64,4,512]{2,0,1:T(8,128)(2,1)S(1)} all-to-all(bf16[64,4,512]{2,0,1:T(8,128)(2,1)S(1)} %bitcast.105), channel_id=1, replica_groups=mesh['ctx'=8,'fsdp'=4] {'fsdp'}, dimensions={1} | all-to-all | bytes 524288 | tf_op jit(solution)/shard_map/all_to_all | solution.py:182
  85.7 18.3 %all_to_all.87 = bf16[64,4,1408]{2,0,1:T(8,128)(2,1)S(1)} all-to-all(bf16[64,4,1408]{2,0,1:T(8,128)(2,1)S(1)} %bitcast.98), channel_id=1, replica_groups=mesh['ctx'=8,'fsdp'=4] {'fsdp'}, dimensions={1} | all-to-all | bytes 1441792 | tf_op jit(solution)/shard_map/all_to_all | solution.py:182
  108.4 15.6 %attend_forward.1 = bf16[512,512]{1,0:T(8,128)(2,1)} custom-call(bf16[512,512]{1,0:T(8,128)(2,1)} %bitcast.113, bf16[8,128,512]{2,1,0:T(8,128)(2,1)} %bitcast.135, f32[1024,128]{1,0:T(8,128)} %compare_select_fusion.bias_ref), custom_call_target="tpu_custom_call" | custom-call | flops 1073741824 | bytes 2097152 | tf_op jit(solution)/shard_map/attend_forward/pallas_call | solution.py:112
  134.9 11.4 %collective-permute-done.3 = bf16[128,2048]{1,0:T(8,128)(2,1)S(1)} collective-permute-done((bf16[128,2048]{1,0:T(8,128)(2,1)S(1)}, bf16[128,2048]{1,0:T(8,128)(2,1)S(1)}, u32[]{:S(2)}, u32[]{:S(2)}) %collective-permute-start.3) | collective-permute-done | bytes 524320 | tf_op jit(solution)/shard_map/ppermute | solution.py:174
  146.3 21.7 %collective-permute-done.4 = bf16[128,2048]{1,0:T(8,128)(2,1)S(1)} collective-permute-done((bf16[128,2048]{1,0:T(8,128)(2,1)S(1)}, bf16[128,2048]{1,0:T(8,128)(2,1)S(1)}, u32[]{:S(2)}, u32[]{:S(2)}) %collective-permute-start.4) | collective-permute-done | bytes 524320 | tf_op jit(solution)/shard_map/ppermute | solution.py:174
  168.8 12.7 %collective-permute-start.6 = (bf16[128,2048]{1,0:T(8,128)(2,1)S(1)}, bf16[128,2048]{1,0:T(8,128)(2,1)S(1)}, u32[]{:S(2)}, u32[]{:S(2)}) collective-permute-start(bf16[128,2048]{1,0:T(8,128)(2,1)S(1)} %multiply_convert_fusion.3), channel_id=1, source_target_pairs={{1,0},{2,1},{3,2},{0,3},{5,4},{6,5},{7,6},{4,7},{9,8},{10,9},{11,1... | collective-permute-start | bytes 1572872 | tf_op jit(solution)/shard_map/ppermute | solution.py:168
  182.2 3.7 collective-permute-start.12
  186.6 7.2 collective-permute-done.6
  193.8 24.0 %collective-permute-start.14 = (bf16[128,2048]{1,0:T(8,128)(2,1)S(1)}, bf16[128,2048]{1,0:T(8,128)(2,1)}, u32[]{:S(2)}, u32[]{:S(2)}) collective-permute-start(bf16[128,2048]{1,0:T(8,128)(2,1)S(1)} %bitcast.109), channel_id=1, source_target_pairs={{3,0},{0,1},{1,2},{2,3},{7,4},{4,5},{5,6},{6,7},{11,8},{8,9},{9,10... | collective-permute-start | bytes 1572872 | tf_op jit(solution)/shard_map/ppermute | solution.py:168
  217.8 33.1 %collective-permute-done.7 = bf16[128,2048]{1,0:T(8,128)(2,1)S(1)} collective-permute-done((bf16[128,2048]{1,0:T(8,128)(2,1)S(1)}, bf16[128,2048]{1,0:T(8,128)(2,1)S(1)}, u32[]{:S(2)}, u32[]{:S(2)}) %collective-permute-start.7) | collective-permute-done | bytes 524320 | tf_op jit(solution)/shard_map/ppermute | solution.py:168
  251.0 5.1 fusion.34
  256.1 5.1 fusion.35
  261.2 3.5 copy.37
  264.7 7.9 collective-permute-done.13
  272.6 5.9 multiply_convert_fusion
  278.6 3.5 fusion.50
  282.1 5.8 fusion.47
  292.0 3.4 fusion.48
  298.5 6.2 collective-permute-done.15
  304.8 41.6 %collective-permute-start.9 = (bf16[128,2048]{1,0:T(8,128)(2,1)S(1)}, bf16[128,2048]{1,0:T(8,128)(2,1)S(1)}, u32[]{:S(2)}, u32[]{:S(2)}) collective-permute-start(bf16[128,2048]{1,0:T(8,128)(2,1)S(1)} %get-tuple-element.67), channel_id=1, source_target_pairs={{0,1},{1,2},{2,3},{3,0},{4,5},{5,6},{6,7},{7,4},{8,9},{9,10},{10,1... | collective-permute-start | bytes 1572872 | tf_op jit(solution)/shard_map/ppermute | solution.py:174
  347.0 23.4 %collective-permute-done.10 = bf16[128,2048]{1,0:T(8,128)(2,1)S(1)} collective-permute-done((bf16[128,2048]{1,0:T(8,128)(2,1)S(1)}, bf16[128,2048]{1,0:T(8,128)(2,1)S(1)}, u32[]{:S(2)}, u32[]{:S(2)}) %collective-permute-start.10) | collective-permute-done | bytes 524320 | tf_op jit(solution)/shard_map/ppermute | solution.py:174
  372.4 11.1 %collective-permute-start.18 = (bf16[128,2048]{1,0:T(8,128)(2,1)S(1)}, bf16[128,2048]{1,0:T(8,128)(2,1)S(1)}, u32[]{:S(2)}, u32[]{:S(2)}) collective-permute-start(bf16[128,2048]{1,0:T(8,128)(2,1)S(1)} %get-tuple-element.51), channel_id=1, source_target_pairs={{1,0},{2,1},{3,2},{0,3},{5,4},{6,5},{7,6},{4,7},{9,8},{10,9},{11,1... | collective-permute-start | bytes 1572872 | tf_op jit(solution)/shard_map/ppermute | solution.py:168
  383.5 4.8 collective-permute-start.19
  390.3 6.9 collective-permute-done.18
  397.2 35.2 %collective-permute-done.19 = bf16[128,2048]{1,0:T(8,128)(2,1)S(1)} collective-permute-done((bf16[128,2048]{1,0:T(8,128)(2,1)S(1)}, bf16[128,2048]{1,0:T(8,128)(2,1)S(1)}, u32[]{:S(2)}, u32[]{:S(2)}) %collective-permute-start.19) | collective-permute-done | bytes 524320 | tf_op jit(solution)/shard_map/ppermute | solution.py:168
  436.2 23.1 %attend_backward.1 = (bf16[512,512]{1,0:T(8,128)(2,1)}, bf16[8,128,512]{2,1,0:T(8,128)(2,1)}) custom-call(bf16[512,512]{1,0:T(8,128)(2,1)} %bitcast.114, bf16[8,128,512]{2,1,0:T(8,128)(2,1)} %bitcast.136, f32[1024,128]{1,0:T(8,128)} %compare_select_fusion.bias_ref, bf16[512,512]{1,0:T(8,128)(2,1)} %convolution_convert_fusion.5.do_ref, f32[32,128]{1,0:T(8,128)} %copy-done.22, ...), custom_call_target="tpu_custom_call" | custom-call | flops 2684354560 | bytes 3670016 | tf_op jit(solution)/shard_map/attend_backward/pallas_call | solution.py:141
  459.4 5.5 convolution_convert_fusion
  464.9 6.9 copy.42
  477.6 15.1 %reduce-scatter.5.cloned.1.call-done = bf16[1,128,512]{2,1,0:T(8,128)(2,1)} async-done(((bf16[8,128,512]{2,1,0:T(8,128)(2,1)}), bf16[1,128,512]{2,1,0:T(8,128)(2,1)}) %reduce-scatter.5.cloned.1.call-update) | async-done | bytes 131088 | tf_op jit(solution)/shard_map/reduce_scatter | solution.py:319
  493.8 4.5 convolution_convert_fusion.3
  498.6 7.1 convolution_convert_fusion.1
  506.8 6.4 convolution_convert_fusion.2
  515.0 5.7 fusion.49
  520.7 96.5 %all-reduce.5.cloned.1.call-done = (bf16[4,512,512]{2,0,1:T(4,128)(2,1)}, bf16[4,512,1408]{2,0,1:T(4,128)(2,1)}) async-done(((bf16[4,512,512]{2,0,1:T(4,128)(2,1)}, bf16[4,512,1408]{2,0,1:T(4,128)(2,1)}), (bf16[4,512,512]{2,0,1:T(4,128)(2,1)}, bf16[4,512,1408]{2,0,1:T(4,128)(2,1)})) %all-reduce.5.cloned.1.call-update) | async-done | bytes 7864336
  619.0 4.6 all-to-all-start.2
  633.0 22.4 %all-to-all-done.2 = bf16[4,64,512]{2,1,0:T(8,128)(2,1)S(1)} async-done(((bf16[4,64,512]{2,1,0:T(8,128)(2,1)}), bf16[4,64,512]{2,1,0:T(8,128)(2,1)S(1)}, u32[]{:S(2)}, u32[]{:S(2)}) %all-to-all-start.2) | async-done | bytes 262176 | tf_op jit(solution)/shard_map/all_to_all | solution.py:192
  656.2 3.5 all-to-all-start.4
  659.7 10.9 %collective-permute-done.22 = bf16[128,2048]{1,0:T(8,128)(2,1)S(1)} collective-permute-done((bf16[128,2048]{1,0:T(8,128)(2,1)}, bf16[128,2048]{1,0:T(8,128)(2,1)S(1)}, u32[]{:S(2)}, u32[]{:S(2)}) %collective-permute-start.22) | collective-permute-done | bytes 524320 | tf_op jit(solution)/shard_map/ppermute | solution.py:174
  673.9 54.0 %psum.7 = f32[2,2048]{1,0:T(2,128)S(1)} all-reduce(f32[2,2048]{1,0:T(2,128)S(1)} %pad_maximum_fusion.14), channel_id=1, replica_groups=mesh['ctx'=8,'fsdp'=4] {'ctx','fsdp'}, use_global_device_ids=true, to_apply=%region_8.9 | all-reduce | flops 4096 | bytes 32768 | tf_op jit(solution)/shard_map/psum | solution.py:344
  728.9 4.1 all-to-all-start.3
  740.1 3.6 all-to-all-start.5
  750.0 6.2 all-to-all-done.5
  757.5 3.1 copy.46
  762.9 26.9 %reduce-scatter.9.cloned.1.call-done = bf16[1408,256]{1,0:T(8,128)(2,1)} async-done(((bf16[1408,2048]{1,0:T(8,128)(2,1)}), bf16[1408,256]{1,0:T(8,128)(2,1)}) %reduce-scatter.9.cloned.1.call-update) | async-done | bytes 720912 | tf_op jit(solution)/shard_map/reduce_scatter | solution.py:349
  (233 shorter events, 87.4 us)
Async XLA Ops:
  7.2 66.8 %copy-start = (bf16[512,2048]{1,0:T(8,128)(2,1)S(1)}, bf16[512,2048]{1,0:T(8,128)(2,1)}, u32[]{:S(2)}) copy-start(bf16[512,2048]{1,0:T(8,128)(2,1)} %param.17) | copy-start | bytes 6291460
  7.2 101.2 %all-gather.7.cloned.1.call-start = ((), (), s32[]{:S(2)}) async-start(), calls=%async_computation.14 | async-start | bytes 1179648 | tf_op jit(solution)/shard_map/all_gather | solution.py:277
  7.3 57.8 %collective-permute-start = (bf16[128,2048]{1,0:T(8,128)(2,1)}, bf16[128,2048]{1,0:T(8,128)(2,1)S(1)}, u32[]{:S(2)}, u32[]{:S(2)}) collective-permute-start(bf16[128,2048]{1,0:T(8,128)(2,1)} %bitcast.85), channel_id=1, source_target_pairs={{1,0},{2,1},{3,2},{0,3},{5,4},{6,5},{7,6},{4,7},{9,8},{10,9},{11,1... | collective-permute-start | bytes 1572872 | tf_op jit(solution)/shard_map/ppermute | solution.py:168
  12.4 52.7 %collective-permute-start.1 = (bf16[128,2048]{1,0:T(8,128)(2,1)}, bf16[128,2048]{1,0:T(8,128)(2,1)}, u32[]{:S(2)}, u32[]{:S(2)}) collective-permute-start(bf16[128,2048]{1,0:T(8,128)(2,1)} %bitcast.86), channel_id=1, source_target_pairs={{2,0},{3,1},{0,2},{1,3},{6,4},{7,5},{4,6},{5,7},{10,8},{11,9},{8,1... | collective-permute-start | bytes 1572872 | tf_op jit(solution)/shard_map/ppermute | solution.py:168
  12.4 52.7 %collective-permute-start.2 = (bf16[128,2048]{1,0:T(8,128)(2,1)}, bf16[128,2048]{1,0:T(8,128)(2,1)}, u32[]{:S(2)}, u32[]{:S(2)}) collective-permute-start(bf16[128,2048]{1,0:T(8,128)(2,1)} %bitcast.87), channel_id=1, source_target_pairs={{3,0},{0,1},{1,2},{2,3},{7,4},{4,5},{5,6},{6,7},{11,8},{8,9},{9,10... | collective-permute-start | bytes 1572872 | tf_op jit(solution)/shard_map/ppermute | solution.py:168
  19.4 87.5 %copy-start.22 = (f32[32,128]{1,0:T(8,128)}, f32[32,128]{1,0:T(8,128)S(1)}, u32[]{:S(2)}) copy-start(f32[32,128]{1,0:T(8,128)S(1)} %get-tuple-element.87.cos_ref) | copy-start | bytes 49156
  19.4 87.5 %copy-start.24 = (f32[32,128]{1,0:T(8,128)}, f32[32,128]{1,0:T(8,128)S(1)}, u32[]{:S(2)}) copy-start(f32[32,128]{1,0:T(8,128)S(1)} %get-tuple-element.88.sin_ref) | copy-start | bytes 49156
  73.9 52.0 %all-gather.9.cloned.1.call-start = ((), (), s32[]{:S(2)}) async-start(), calls=%async_computation.15 | async-start | bytes 2359296 | tf_op jit(solution)/shard_map/all_gather | solution.py:184
  84.4 176.7 %all-gather.11.cloned.1.call-start = ((), (), s32[]{:S(2)}) async-start(), calls=%async_computation.16 | async-start | bytes 6488064 | tf_op jit(solution)/shard_map/all_gather | solution.py:184
  105.5 387.2 %reduce-scatter.5.cloned.1.call-start = ((), (), s32[]{:S(2)}) async-start(), calls=%async_computation.10 | async-start | bytes 1179648 | tf_op jit(solution)/shard_map/reduce_scatter | solution.py:319
  125.9 125.1 %slice-start.5 = ((s8[5767168]{0:T(1024)(128)(4,1)}), s8[4194304]{0:T(1024)(128)(4,1)S(1)}, s32[]{:S(2)}) async-start(s8[5767168]{0:T(1024)(128)(4,1)} %bitcast.133), calls=%async_computation.23 | async-start | bytes 8388608
  128.1 122.9 %slice-start.6 = ((s8[5767168]{0:T(1024)(128)(4,1)}), s8[1572864]{0:T(1024)(128)(4,1)S(1)}, s32[]{:S(2)}) async-start(s8[5767168]{0:T(1024)(128)(4,1)} %bitcast.133), calls=%async_computation.24 | async-start | bytes 3145728
  129.5 16.8 %collective-permute-start.3 = (bf16[128,2048]{1,0:T(8,128)(2,1)S(1)}, bf16[128,2048]{1,0:T(8,128)(2,1)S(1)}, u32[]{:S(2)}, u32[]{:S(2)}) collective-permute-start(bf16[128,2048]{1,0:T(8,128)(2,1)S(1)} %get-tuple-element.70), channel_id=1, source_target_pairs={{0,1},{1,2},{2,3},{3,0},{4,5},{5,6},{6,7},{7,4},{8,9},{9,10},{10,1... | collective-permute-start | bytes 1572872 | tf_op jit(solution)/shard_map/ppermute | solution.py:174
  131.1 37.0 %collective-permute-start.4 = (bf16[128,2048]{1,0:T(8,128)(2,1)S(1)}, bf16[128,2048]{1,0:T(8,128)(2,1)S(1)}, u32[]{:S(2)}, u32[]{:S(2)}) collective-permute-start(bf16[128,2048]{1,0:T(8,128)(2,1)S(1)} %get-tuple-element.72), channel_id=1, source_target_pairs={{0,2},{1,3},{2,0},{3,1},{4,6},{5,7},{6,4},{7,5},{8,10},{9,11},{10,... | collective-permute-start | bytes 1572872 | tf_op jit(solution)/shard_map/ppermute | solution.py:174
  133.5 34.6 %collective-permute-start.5 = (bf16[128,2048]{1,0:T(8,128)(2,1)S(1)}, bf16[128,2048]{1,0:T(8,128)(2,1)S(1)}, u32[]{:S(2)}, u32[]{:S(2)}) collective-permute-start(bf16[128,2048]{1,0:T(8,128)(2,1)S(1)} %get-tuple-element.71), channel_id=1, source_target_pairs={{0,3},{1,0},{2,1},{3,2},{4,7},{5,4},{6,5},{7,6},{8,11},{9,8},{10,9... | collective-permute-start | bytes 1572872 | tf_op jit(solution)/shard_map/ppermute | solution.py:174
  168.8 87.3 %copy-start.20 = (bf16[128,2048]{1,0:T(8,128)(2,1)}, bf16[128,2048]{1,0:T(8,128)(2,1)S(1)}, u32[]{:S(2)}) copy-start(bf16[128,2048]{1,0:T(8,128)(2,1)S(1)} %multiply_convert_fusion.3) | copy-start | bytes 1572868
  168.8 25.0 %collective-permute-start.6 = (bf16[128,2048]{1,0:T(8,128)(2,1)S(1)}, bf16[128,2048]{1,0:T(8,128)(2,1)S(1)}, u32[]{:S(2)}, u32[]{:S(2)}) collective-permute-start(bf16[128,2048]{1,0:T(8,128)(2,1)S(1)} %multiply_convert_fusion.3), channel_id=1, source_target_pairs={{1,0},{2,1},{3,2},{0,3},{5,4},{6,5},{7,6},{4,7},{9,8},{10,9},{11,1... | collective-permute-start | bytes 1572872 | tf_op jit(solution)/shard_map/ppermute | solution.py:168
  181.4 69.5 %collective-permute-start.7 = (bf16[128,2048]{1,0:T(8,128)(2,1)S(1)}, bf16[128,2048]{1,0:T(8,128)(2,1)S(1)}, u32[]{:S(2)}, u32[]{:S(2)}) collective-permute-start(bf16[128,2048]{1,0:T(8,128)(2,1)S(1)} %multiply_convert_fusion.3), channel_id=1, source_target_pairs={{2,0},{3,1},{0,2},{1,3},{6,4},{7,5},{4,6},{5,7},{10,8},{11,9},{8,1... | collective-permute-start | bytes 1572872 | tf_op jit(solution)/shard_map/ppermute | solution.py:168
  182.0 69.0 %collective-permute-start.8 = (bf16[128,2048]{1,0:T(8,128)(2,1)S(1)}, bf16[128,2048]{1,0:T(8,128)(2,1)S(1)}, u32[]{:S(2)}, u32[]{:S(2)}) collective-permute-start(bf16[128,2048]{1,0:T(8,128)(2,1)S(1)} %multiply_convert_fusion.3), channel_id=1, source_target_pairs={{3,0},{0,1},{1,2},{2,3},{7,4},{4,5},{5,6},{6,7},{11,8},{8,9},{9,10... | collective-permute-start | bytes 1572872 | tf_op jit(solution)/shard_map/ppermute | solution.py:168
  182.2 73.8 %slice-start.1 = ((s8[5767168]{0:T(1024)(128)(4,1)}), s8[4194304]{0:T(1024)(128)(4,1)S(1)}, s32[]{:S(2)}) async-start(s8[5767168]{0:T(1024)(128)(4,1)} %bitcast.129), calls=%async_computation.19 | async-start | bytes 8388608
  182.2 73.8 %slice-start.2 = ((s8[5767168]{0:T(1024)(128)(4,1)}), s8[1572864]{0:T(1024)(128)(4,1)S(1)}, s32[]{:S(2)}) async-start(s8[5767168]{0:T(1024)(128)(4,1)} %bitcast.129), calls=%async_computation.20 | async-start | bytes 3145728
  182.2 82.4 %collective-permute-start.12 = (bf16[128,2048]{1,0:T(8,128)(2,1)S(1)}, bf16[128,2048]{1,0:T(8,128)(2,1)}, u32[]{:S(2)}, u32[]{:S(2)}) collective-permute-start(bf16[128,2048]{1,0:T(8,128)(2,1)S(1)} %bitcast.107), channel_id=1, source_target_pairs={{1,0},{2,1},{3,2},{0,3},{5,4},{6,5},{7,6},{4,7},{9,8},{10,9},{11,1... | collective-permute-start | bytes 1572872 | tf_op jit(solution)/shard_map/ppermute | solution.py:168
  186.0 86.6 %collective-permute-start.13 = (bf16[128,2048]{1,0:T(8,128)(2,1)S(1)}, bf16[128,2048]{1,0:T(8,128)(2,1)}, u32[]{:S(2)}, u32[]{:S(2)}) collective-permute-start(bf16[128,2048]{1,0:T(8,128)(2,1)S(1)} %bitcast.108), channel_id=1, source_target_pairs={{2,0},{3,1},{0,2},{1,3},{6,4},{7,5},{4,6},{5,7},{10,8},{11,9},{8,1... | collective-permute-start | bytes 1572872 | tf_op jit(solution)/shard_map/ppermute | solution.py:168
  193.8 62.2 %copy-start.28 = (bf16[128,2048]{1,0:T(8,128)(2,1)}, bf16[128,2048]{1,0:T(8,128)(2,1)S(1)}, u32[]{:S(2)}) copy-start(bf16[128,2048]{1,0:T(8,128)(2,1)S(1)} %collective-permute-done.6) | copy-start | bytes 1572868
  193.8 78.8 %collective-permute-start.14 = (bf16[128,2048]{1,0:T(8,128)(2,1)S(1)}, bf16[128,2048]{1,0:T(8,128)(2,1)}, u32[]{:S(2)}, u32[]{:S(2)}) collective-permute-start(bf16[128,2048]{1,0:T(8,128)(2,1)S(1)} %bitcast.109), channel_id=1, source_target_pairs={{3,0},{0,1},{1,2},{2,3},{7,4},{4,5},{5,6},{6,7},{11,8},{8,9},{9,10... | collective-permute-start | bytes 1572872 | tf_op jit(solution)/shard_map/ppermute | solution.py:168
  288.0 16.7 %collective-permute-start.15 = (bf16[128,2048]{1,0:T(8,128)(2,1)S(1)}, bf16[128,2048]{1,0:T(8,128)(2,1)S(1)}, u32[]{:S(2)}, u32[]{:S(2)}) collective-permute-start(bf16[128,2048]{1,0:T(8,128)(2,1)S(1)} %get-tuple-element.64), channel_id=1, source_target_pairs={{0,1},{1,2},{2,3},{3,0},{4,5},{5,6},{6,7},{7,4},{8,9},{9,10},{10,1... | collective-permute-start | bytes 1572872 | tf_op jit(solution)/shard_map/ppermute | solution.py:174
  288.1 58.3 %collective-permute-start.16 = (bf16[128,2048]{1,0:T(8,128)(2,1)S(1)}, bf16[128,2048]{1,0:T(8,128)(2,1)S(1)}, u32[]{:S(2)}, u32[]{:S(2)}) collective-permute-start(bf16[128,2048]{1,0:T(8,128)(2,1)S(1)} %get-tuple-element.66), channel_id=1, source_target_pairs={{0,2},{1,3},{2,0},{3,1},{4,6},{5,7},{6,4},{7,5},{8,10},{9,11},{10,... | collective-permute-start | bytes 1572872 | tf_op jit(solution)/shard_map/ppermute | solution.py:174
  289.1 57.3 %collective-permute-start.17 = (bf16[128,2048]{1,0:T(8,128)(2,1)S(1)}, bf16[128,2048]{1,0:T(8,128)(2,1)S(1)}, u32[]{:S(2)}, u32[]{:S(2)}) collective-permute-start(bf16[128,2048]{1,0:T(8,128)(2,1)S(1)} %get-tuple-element.65), channel_id=1, source_target_pairs={{0,3},{1,0},{2,1},{3,2},{4,7},{5,4},{6,5},{7,6},{8,11},{9,8},{10,9... | collective-permute-start | bytes 1572872 | tf_op jit(solution)/shard_map/ppermute | solution.py:174
  295.6 74.9 %copy-start.11 = (bf16[1,128,2048]{2,1,0:T(8,128)(2,1)S(1)}, bf16[1,128,2048]{2,1,0:T(8,128)(2,1)}, u32[]{:S(2)}) copy-start(bf16[1,128,2048]{2,1,0:T(8,128)(2,1)} %param.21) | copy-start | bytes 1572868
  295.6 74.8 %collective-permute-start.10 = (bf16[128,2048]{1,0:T(8,128)(2,1)S(1)}, bf16[128,2048]{1,0:T(8,128)(2,1)S(1)}, u32[]{:S(2)}, u32[]{:S(2)}) collective-permute-start(bf16[128,2048]{1,0:T(8,128)(2,1)S(1)} %get-tuple-element.69), channel_id=1, source_target_pairs={{0,2},{1,3},{2,0},{3,1},{4,6},{5,7},{6,4},{7,5},{8,10},{9,11},{10,... | collective-permute-start | bytes 1572872 | tf_op jit(solution)/shard_map/ppermute | solution.py:174
  297.6 72.8 %collective-permute-start.11 = (bf16[128,2048]{1,0:T(8,128)(2,1)S(1)}, bf16[128,2048]{1,0:T(8,128)(2,1)S(1)}, u32[]{:S(2)}, u32[]{:S(2)}) collective-permute-start(bf16[128,2048]{1,0:T(8,128)(2,1)S(1)} %get-tuple-element.68), channel_id=1, source_target_pairs={{0,3},{1,0},{2,1},{3,2},{4,7},{5,4},{6,5},{7,6},{8,11},{9,8},{10,9... | collective-permute-start | bytes 1572872 | tf_op jit(solution)/shard_map/ppermute | solution.py:174
  304.8 65.7 %collective-permute-start.9 = (bf16[128,2048]{1,0:T(8,128)(2,1)S(1)}, bf16[128,2048]{1,0:T(8,128)(2,1)S(1)}, u32[]{:S(2)}, u32[]{:S(2)}) collective-permute-start(bf16[128,2048]{1,0:T(8,128)(2,1)S(1)} %get-tuple-element.67), channel_id=1, source_target_pairs={{0,1},{1,2},{2,3},{3,0},{4,5},{5,6},{6,7},{7,4},{8,9},{9,10},{10,1... | collective-permute-start | bytes 1572872 | tf_op jit(solution)/shard_map/ppermute | solution.py:174
  370.5 63.6 %copy-start.4 = (bf16[4,512,1,512]{3,1,0,2:T(8,128)(2,1)S(1)}, bf16[4,512,1,512]{3,1,0,2:T(8,128)(2,1)}, u32[]{:S(2)}) copy-start(bf16[4,512,1,512]{3,1,0,2:T(8,128)(2,1)} %copy-done.3) | copy-start | bytes 6291460
  372.4 24.8 %collective-permute-start.18 = (bf16[128,2048]{1,0:T(8,128)(2,1)S(1)}, bf16[128,2048]{1,0:T(8,128)(2,1)S(1)}, u32[]{:S(2)}, u32[]{:S(2)}) collective-permute-start(bf16[128,2048]{1,0:T(8,128)(2,1)S(1)} %get-tuple-element.51), channel_id=1, source_target_pairs={{1,0},{2,1},{3,2},{0,3},{5,4},{6,5},{7,6},{4,7},{9,8},{10,9},{11,1... | collective-permute-start | bytes 1572872 | tf_op jit(solution)/shard_map/ppermute | solution.py:168
  383.5 48.9 %collective-permute-start.19 = (bf16[128,2048]{1,0:T(8,128)(2,1)S(1)}, bf16[128,2048]{1,0:T(8,128)(2,1)S(1)}, u32[]{:S(2)}, u32[]{:S(2)}) collective-permute-start(bf16[128,2048]{1,0:T(8,128)(2,1)S(1)} %get-tuple-element.51), channel_id=1, source_target_pairs={{2,0},{3,1},{0,2},{1,3},{6,4},{7,5},{4,6},{5,7},{10,8},{11,9},{8,1... | collective-permute-start | bytes 1572872 | tf_op jit(solution)/shard_map/ppermute | solution.py:168
  388.3 44.1 %collective-permute-start.20 = (bf16[128,2048]{1,0:T(8,128)(2,1)S(1)}, bf16[128,2048]{1,0:T(8,128)(2,1)S(1)}, u32[]{:S(2)}, u32[]{:S(2)}) collective-permute-start(bf16[128,2048]{1,0:T(8,128)(2,1)S(1)} %get-tuple-element.51), channel_id=1, source_target_pairs={{3,0},{0,1},{1,2},{2,3},{7,4},{4,5},{5,6},{6,7},{11,8},{8,9},{9,10... | collective-permute-start | bytes 1572872 | tf_op jit(solution)/shard_map/ppermute | solution.py:168
  459.3 157.9 %all-reduce.5.cloned.1.call-start = ((), (), s32[]{:S(2)}) async-start(), calls=%async_computation.17 | async-start | bytes 15728640
  477.5 269.3 %reduce-scatter.7.cloned.1.call-start = ((), (), s32[]{:S(2)}) async-start(), calls=%async_computation.11 | async-start | bytes 2949120 | tf_op jit(solution)/shard_map/reduce_scatter | solution.py:349
  498.3 262.3 %reduce-scatter.11.cloned.1.call-start = ((), (), s32[]{:S(2)}) async-start(), calls=%async_computation.13 | async-start | bytes 6488064 | tf_op jit(solution)/shard_map/reduce_scatter | solution.py:349
  505.7 284.1 %reduce-scatter.9.cloned.1.call-start = ((), (), s32[]{:S(2)}) async-start(), calls=%async_computation.12 | async-start | bytes 6488064 | tf_op jit(solution)/shard_map/reduce_scatter | solution.py:349
  619.0 36.4 %all-to-all-start.2 = ((bf16[4,64,512]{2,1,0:T(8,128)(2,1)}), bf16[4,64,512]{2,1,0:T(8,128)(2,1)S(1)}, u32[]{:S(2)}, u32[]{:S(2)}) async-start(bf16[4,64,512]{2,1,0:T(8,128)(2,1)} %copy.39), calls=%async_computation.4 | async-start | bytes 524288 | tf_op jit(solution)/shard_map/all_to_all | solution.py:192
  624.8 34.9 %collective-permute-start.21 = (bf16[128,2048]{1,0:T(8,128)(2,1)}, bf16[128,2048]{1,0:T(8,128)(2,1)S(1)}, u32[]{:S(2)}, u32[]{:S(2)}) collective-permute-start(bf16[128,2048]{1,0:T(8,128)(2,1)} %get-tuple-element.61), channel_id=1, source_target_pairs={{0,1},{1,2},{2,3},{3,0},{4,5},{5,6},{6,7},{7,4},{8,9},{9,10},{10,1... | collective-permute-start | bytes 1572872 | tf_op jit(solution)/shard_map/ppermute | solution.py:174
  626.8 43.8 %collective-permute-start.22 = (bf16[128,2048]{1,0:T(8,128)(2,1)}, bf16[128,2048]{1,0:T(8,128)(2,1)S(1)}, u32[]{:S(2)}, u32[]{:S(2)}) collective-permute-start(bf16[128,2048]{1,0:T(8,128)(2,1)} %get-tuple-element.63), channel_id=1, source_target_pairs={{0,2},{1,3},{2,0},{3,1},{4,6},{5,7},{6,4},{7,5},{8,10},{9,11},{10,... | collective-permute-start | bytes 1572872 | tf_op jit(solution)/shard_map/ppermute | solution.py:174
  629.2 41.4 %collective-permute-start.23 = (bf16[128,2048]{1,0:T(8,128)(2,1)}, bf16[128,2048]{1,0:T(8,128)(2,1)}, u32[]{:S(2)}, u32[]{:S(2)}) collective-permute-start(bf16[128,2048]{1,0:T(8,128)(2,1)} %get-tuple-element.62), channel_id=1, source_target_pairs={{0,3},{1,0},{2,1},{3,2},{4,7},{5,4},{6,5},{7,6},{8,11},{9,8},{10,9... | collective-permute-start | bytes 1572872 | tf_op jit(solution)/shard_map/ppermute | solution.py:174
  656.2 72.8 %all-to-all-start.4 = ((bf16[4,64,1408]{2,1,0:T(8,128)(2,1)}), bf16[4,64,1408]{2,1,0:T(8,128)(2,1)S(1)}, u32[]{:S(2)}, u32[]{:S(2)}) async-start(bf16[4,64,1408]{2,1,0:T(8,128)(2,1)} %copy.43), calls=%async_computation.8 | async-start | bytes 1441792 | tf_op jit(solution)/shard_map/all_to_all | solution.py:192
  659.6 68.3 %copy-start.9 = (bf16[4,64,512]{2,1,0:T(8,128)(2,1)S(1)}, bf16[4,64,512]{2,1,0:T(8,128)(2,1)}, u32[]{:S(2)}) copy-start(bf16[4,64,512]{2,1,0:T(8,128)(2,1)} %copy-done.8) | copy-start | bytes 786436
  728.9 11.2 %all-to-all-start.3 = ((bf16[64,8,256]{2,0,1:T(8,128)(2,1)}), bf16[64,8,256]{2,0,1:T(8,128)(2,1)}, u32[]{:S(2)}, u32[]{:S(2)}) async-start(bf16[64,8,256]{2,0,1:T(8,128)(2,1)} %copy.41), calls=%async_computation.5 | async-start | bytes 524288 | tf_op jit(solution)/shard_map/all_to_all | solution.py:194
  740.1 16.1 %all-to-all-start.5 = ((bf16[64,8,704]{2,0,1:T(8,128)(2,1)}), bf16[64,8,704]{2,0,1:T(8,128)(2,1)S(1)}, u32[]{:S(2)}, u32[]{:S(2)}) async-start(bf16[64,8,704]{2,0,1:T(8,128)(2,1)} %copy.45), calls=%async_computation.9 | async-start | bytes 1572864 | tf_op jit(solution)/shard_map/all_to_all | solution.py:194
  (40 other events, 502.4 us)
Sparse Core Ops, SparseCore 0:
  74.0 21.5 all-gather.6
  98.1 27.7 all-gather.8
  128.4 43.2 all-gather.10
  459.5 33.1 reduce-scatter.4
  495.9 121.2 all-reduce.4
  620.4 43.6 reduce-scatter.6
  667.5 59.6 reduce-scatter.10
  730.6 59.2 reduce-scatter.8

commit v2 on v1

v2 whole, which is shorter than its diff:
```python
import jax
import jax.numpy as jnp
from jax import lax
from jax.experimental import pallas as pl
from jax.experimental.pallas import tpu as pltpu
from jax.sharding import PartitionSpec as P

KV_HEADS = 4
HEAD_DIM = 64
HALF_DIM = HEAD_DIM // 2

rms_eps = 1e-05
rope_base = 10000.0
masked_score = -1e30
score_scale = HEAD_DIM ** (-0.5)


f32 = jnp.float32
bf16 = jnp.bfloat16


def dot(a, b, ca, cb):
    return lax.dot_general(a, b, (((ca,), (cb,)), ((), ())), preferred_element_type=f32)


def unpack_keys(kv_ref, kn, vn, kt, vt):
    blocks, _, tokens = kv_ref.shape
    for b in range(blocks):
        span = slice(b * tokens, (b + 1) * tokens)
        both = kv_ref[b]
        kt[:, span] = both[:HEAD_DIM]
        vt[:, span] = both[HEAD_DIM:]
        turned = both.T
        kn[span, :] = turned[:, :HEAD_DIM]
        vn[span, :] = turned[:, HEAD_DIM:]


def attend_forward_body(q_ref, kv_ref, bias_ref, o_ref, kn, vn, kt, vt):
    unpack_keys(kv_ref, kn, vn, kt, vt)
    heads = q_ref.shape[0] // HEAD_DIM
    bias = jnp.concatenate([bias_ref[...], bias_ref[...]], axis=1)
    tokens = q_ref.shape[1]
    for h in range(0, heads, 2):
        rows = [slice((h + i) * HEAD_DIM, (h + i + 1) * HEAD_DIM) for i in range(2)]
        q2 = jnp.concatenate([q_ref[r, :] for r in rows], axis=1)
        s = dot(kn[...], q2, 1, 0) + bias
        e = jnp.exp(s - jnp.max(s, axis=0, keepdims=True))
        inv = 1.0 / jnp.sum(e, axis=0, keepdims=True)
        o = dot(vt[...], (e * inv).astype(bf16), 1, 0)
        for i in range(2):
            o_ref[rows[i], :] = o[:, i * tokens : (i + 1) * tokens].astype(bf16)


def attend_backward_body(
    q_ref, kv_ref, bias_ref, do_ref, cos_ref, sin_ref, dq_ref, dkv_ref, kn, vn, kt, vt, dk, dv
):
    unpack_keys(kv_ref, kn, vn, kt, vt)
    heads = q_ref.shape[0] // HEAD_DIM
    bias = jnp.concatenate([bias_ref[...], bias_ref[...]], axis=1)
    tokens = q_ref.shape[1]
    cosine, sine = cos_ref[...], sin_ref[...]
    for h in range(0, heads, 2):
        rows = [slice((h + i) * HEAD_DIM, (h + i + 1) * HEAD_DIM) for i in range(2)]
        q2 = jnp.concatenate([q_ref[r, :] for r in rows], axis=1)
        do2 = jnp.concatenate([do_ref[r, :] for r in rows], axis=1)
        q_flat = jnp.concatenate([q_ref[r, :].T for r in rows], axis=0)
        do_flat = jnp.concatenate([do_ref[r, :].T for r in rows], axis=0)
        s = dot(kn[...], q2, 1, 0) + bias
        e = jnp.exp(s - jnp.max(s, axis=0, keepdims=True))
        p = e * (1.0 / jnp.sum(e, axis=0, keepdims=True))
        dp = dot(vn[...], do2, 1, 0)
        delta = jnp.sum(dp * p, axis=0, keepdims=True)
        ds = (p * (dp - delta)).astype(bf16)
        dv_part = dot(p.astype(bf16), do_flat, 1, 0)
        dk_part = dot(ds, q_flat, 1, 0)
        if h == 0:
            dk[...] = dk_part
            dv[...] = dv_part
        else:
            dk[...] += dk_part
            dv[...] += dv_part
        dq2 = dot(kt[...], ds, 1, 0) * score_scale
        for i in range(2):
            dq = dq2[:, i * tokens : (i + 1) * tokens]
            top, low = dq[:HALF_DIM], dq[HALF_DIM:]
            start = (h + i) * HEAD_DIM
            dq_ref[start : start + HALF_DIM, :] = (top * cosine + low * sine).astype(bf16)
            dq_ref[start + HALF_DIM : start + HEAD_DIM, :] = (low * cosine - top * sine).astype(bf16)
    blocks = kv_ref.shape[0]
    for b in range(blocks):
        span = slice(b * tokens, (b + 1) * tokens)
        dkv_ref[b, :HEAD_DIM, :] = dk[span, :].T.astype(bf16)
        dkv_ref[b, HEAD_DIM:, :] = dv[span, :].T.astype(bf16)


def key_scratch(keys):
    return [
        pltpu.VMEM((keys, HEAD_DIM), bf16),
        pltpu.VMEM((keys, HEAD_DIM), bf16),
        pltpu.VMEM((HEAD_DIM, keys), bf16),
        pltpu.VMEM((HEAD_DIM, keys), bf16),
    ]


def attend_forward(q, kv, bias):
    blocks, both, _ = kv.shape
    keys, tokens = bias.shape
    rows, columns = q.shape
    pieces = columns // tokens
    across = pl.BlockSpec((rows, tokens), lambda g: (0, g))
    elements = pieces * (rows // HEAD_DIM) * tokens * keys
    return pl.pallas_call(
        attend_forward_body,
        out_shape=jax.ShapeDtypeStruct(q.shape, bf16),
        grid=(pieces,),
        in_specs=[
            across,
            pl.BlockSpec((blocks, both, tokens), lambda g: (0, 0, g)),
            pl.BlockSpec((keys, tokens), lambda g: (0, 0)),
        ],
        out_specs=across,
        scratch_shapes=key_scratch(keys),
        cost_estimate=pl.CostEstimate(
            flops=4 * elements * HEAD_DIM,
            bytes_accessed=4 * q.size + 2 * kv.size,
            transcendentals=elements,
        ),
        name="attend_forward",
    )(q, kv, bias)


def attend_backward(q, kv, bias, d_out, cosine, sine, first, earlier):
    blocks, both, _ = kv.shape
    keys, tokens = bias.shape
    rows = q.shape[0]
    pieces = d_out.shape[1] // tokens
    across = pl.BlockSpec((rows, tokens), lambda g: (0, g + first if first else g))
    whole = pl.BlockSpec((blocks, both, tokens), lambda g: (0, 0, g + first if first else g))
    table = pl.BlockSpec((HALF_DIM, tokens), lambda g: (0, 0))
    in_specs = [
        across,
        whole,
        pl.BlockSpec((keys, tokens), lambda g: (0, 0)),
        pl.BlockSpec((rows, tokens), lambda g: (0, g)),
        table,
        table,
    ]
    operands = [q, kv, bias, d_out, cosine, sine]
    aliases, body = {}, attend_backward_body
    if earlier is not None:
        in_specs += [pl.BlockSpec(memory_space=pl.ANY)] * 2
        aliases = {6: 0, 7: 1}
        operands += list(earlier)

        def body(*refs):
            attend_backward_body(*refs[:6], *refs[8:])

    elements = pieces * (rows // HEAD_DIM) * tokens * keys
    return pl.pallas_call(
        body,
        out_shape=(jax.ShapeDtypeStruct(q.shape, bf16), jax.ShapeDtypeStruct(kv.shape, bf16)),
        grid=(pieces,),
        in_specs=in_specs,
        out_specs=(across, whole),
        scratch_shapes=key_scratch(keys)
        + [pltpu.VMEM((keys, HEAD_DIM), f32), pltpu.VMEM((keys, HEAD_DIM), f32)],
        input_output_aliases=aliases,
        cost_estimate=pl.CostEstimate(
            flops=10 * elements * HEAD_DIM,
            bytes_accessed=(6 * q.size + 4 * kv.size) * tokens * pieces // q.shape[1],
            transcendentals=elements,
        ),
    )(*operands)


def fetch(value, k, size):
    return lax.ppermute(value, "fsdp", [((i + k) % size, i) for i in range(size)])


def give(value, k, size):
    return lax.ppermute(value, "fsdp", [(i, (i + k) % size) for i in range(size)])


def gather_pieces(value, size):
    if size != 4:
        return [value] + [fetch(value, k, size) for k in range(1, size)]
    after_one = fetch(value, 1, 4)
    before_one = fetch(value, 3, 4)
    down = lax.ppermute(after_one, "fsdp", [(1, 0), (2, 1)])
    up = lax.ppermute(before_one, "fsdp", [(1, 2), (2, 3)])
    return [value, after_one, jnp.where(lax.axis_index("fsdp") < 2, down, up), before_one]


def scatter_sum(parts, size):
    total = parts[0].astype(f32)
    if size != 4:
        for k in range(1, size):
            total = total + give(parts[k].astype(bf16), k, size).astype(f32)
        return total
    far = parts[2].astype(bf16)
    up = lax.ppermute(far, "fsdp", [(0, 1), (1, 2)])
    down = lax.ppermute(far, "fsdp", [(3, 2), (2, 1)])
    one = (parts[1].astype(f32) + up.astype(f32)).astype(bf16)
    after_one = give(one, 1, 4)
    one = (parts[3].astype(f32) + down.astype(f32)).astype(bf16)
    before_one = give(one, 3, 4)
    return total + after_one.astype(f32) + before_one.astype(f32)


def swap(value, mask):
    size = lax.axis_size("ctx")
    return lax.ppermute(value, "ctx", [(i, i ^ mask) for i in range(size)])


def masks_of(size, first):
    bits = [1 << i for i in range(1, size.bit_length() - 1)]
    return [1] + bits[::-1] if first else bits + [1]


def block_order_of(size):
    found = [0]
    for mask in masks_of(size, False):
        found = found + [m ^ mask for m in found]
    return found


def ctx_gather(value):
    value = value[None]
    for mask in masks_of(lax.axis_size("ctx"), False):
        value = jnp.concatenate([value, swap(value, mask)], axis=0)
    return value


def ctx_sum_back(value):
    for mask in masks_of(lax.axis_size("ctx"), True):
        half = value.shape[0] // 2
        come = swap(value[half:], mask)
        value = (value[:half].astype(f32) + come.astype(f32)).astype(value.dtype)
    return value[0]


def ctx_sum_exchange(value):
    come = lax.all_to_all(value, "ctx", split_axis=0, concat_axis=0, tiled=True)
    return jnp.sum(come.astype(f32), axis=0).astype(value.dtype)


def ctx_sum_scatter(value):
    size = lax.axis_size("ctx")
    c = lax.axis_index("ctx")

    def halve(v, axis, mask):
        bit = (c // mask) % 2
        kept = lax.dynamic_index_in_dim(v, bit, axis, False)
        sent = lax.dynamic_index_in_dim(v, 1 - bit, axis, False)
        come = swap(sent, mask)
        return (kept.astype(f32) + come.astype(f32)).astype(v.dtype)

    bits = size.bit_length() - 1
    v = value.reshape((2,) * bits + value.shape[1:])
    v = halve(v, bits - 1, 1)
    if bits != 3 or value.shape[1] % 32:
        for axis in range(bits - 2, -1, -1):
            v = halve(v, axis, 1 << (bits - 1 - axis))
        return v
    rows = value.shape[1] // 2
    one, two = halve(v[:, :, :rows], 1, 2), halve(v[:, :, rows:], 0, 4)
    return jnp.concatenate([halve(one, 0, 4), halve(two, 0, 2)], axis=0)


def column_blocks(weight, ctx_size, fsdp_size):
    rows, columns = weight.shape
    share, width = rows // ctx_size, columns // fsdp_size
    part = lax.dynamic_slice_in_dim(weight, lax.axis_index("ctx") * share, share)
    return part.reshape(share, fsdp_size, width).transpose(1, 0, 2)


def swap_blocks(blocks):
    return lax.all_to_all(blocks, "fsdp", split_axis=0, concat_axis=0, tiled=True)


def gather_rows(blocks):
    width = blocks.shape[2]
    return lax.all_gather(blocks, "ctx", axis=0).transpose(1, 0, 2, 3).reshape(-1, width)


def own_rows_of(parts, extra):
    F, share = parts[0].shape[:2]
    C = lax.axis_size("ctx")
    cuts = C // F
    widths = [p.shape[2] // cuts for p in parts]
    total = sum(widths)
    n = extra.shape[1]

    def rows_of(values, columns):
        lead, count = values.shape
        rows = -(-count // columns)
        values = jnp.pad(values, ((0, 0), (0, rows * columns - count)))
        return values.reshape(lead, rows, columns).astype(bf16)

    lines = rows_of(extra, total * cuts)
    come = swap_blocks(jnp.concatenate([jnp.concatenate(parts, axis=2), lines], axis=1))
    summed = jnp.sum(come[:, share:].astype(f32), axis=0).reshape(1, -1)[:, :n]
    pieces, start = [], 0
    for w in widths:
        piece = come[:, :share, start : start + w * cuts].reshape(F, share, cuts, w)
        pieces.append(piece.transpose(0, 2, 1, 3).reshape(C, share, w))
        start += w * cuts
    lines = jnp.broadcast_to(rows_of(summed, total), (C, -(-n // total), total))
    come = lax.all_to_all(
        jnp.concatenate([jnp.concatenate(pieces, axis=2), lines], axis=1),
        "ctx",
        split_axis=0,
        concat_axis=0,
        tiled=True,
    )
    summed = jnp.sum(come[:, share:].astype(f32), axis=0).reshape(-1)[:n]
    results, start = [], 0
    for w in widths:
        results.append(come[:, :share, start : start + w].reshape(C * share, w))
        start += w
    return results, summed


def row_shares(grad, ctx_size, fsdp_size):
    rows, width = grad.shape
    share = rows // (ctx_size * fsdp_size)
    grad = grad.reshape(fsdp_size, ctx_size, share, width).transpose(1, 0, 2, 3)
    return grad.reshape(rows, width)


def joined(parts, axis=0):
    return parts[0] if len(parts) == 1 else jnp.concatenate(parts, axis=axis)


def after(value, *others):
    return lax.optimization_barrier((value,) + others)[0]


def inverse_norm(values):
    return lax.rsqrt(jnp.mean(values * values, axis=-1, keepdims=True) + rms_eps)


def per_device(
    inputs,
    block_order,
    norm_gains,
    w_query,
    w_key,
    w_value,
    w_output,
    w_gate,
    w_up,
    w_down,
    out_grad,
):
    C = lax.axis_size("ctx")
    F = lax.axis_size("fsdp")
    z = lax.axis_index("fsdp")
    c = lax.axis_index("ctx")
    tokens, width = inputs.shape[1:]
    keys = tokens * C
    own_x, own_dy = inputs[0], out_grad[0]
    sharing = max(1, F // KV_HEADS)
    kv_rows = w_key.shape[0]
    q_rows = w_query.shape[0]
    gain_width = norm_gains.shape[1]
    order = [0, 1, 3, 2] if F == 4 else list(range(F))
    attention_groups = [order]
    backward_groups = [order[:3], order[3:]] if F == 4 else [order]
    ffn_groups = [order]

    x_pieces = gather_pieces(own_x, F)
    w_out_blocks = column_blocks(after(w_output, x_pieces[1]), C, F)
    share, _ = w_out_blocks.shape[1:]
    gain_blocks = jnp.broadcast_to(norm_gains[None], (F, 2, gain_width))
    swapped = swap_blocks(jnp.concatenate([w_out_blocks, gain_blocks], axis=1))
    w_out_rows = swapped[:, :share]
    gains = swapped[:, share:].transpose(1, 0, 2).reshape(2, F * gain_width)

    half_len = keys // block_order.shape[0]
    offsets = jnp.arange(half_len, dtype=jnp.int32)
    key_pos = (block_order[:, None] * half_len + offsets[None, :]).reshape(keys)
    query_pos = lax.dynamic_slice_in_dim(key_pos, c * tokens, tokens)
    members = jnp.asarray(block_order_of(C), jnp.int32) ^ c
    key_pos = jnp.take(key_pos.reshape(C, tokens), members, axis=0).reshape(keys)
    bias = jnp.where(key_pos[:, None] <= query_pos[None, :], 0.0, masked_score).astype(f32)
    frequency = rope_base ** (-jnp.arange(0, HEAD_DIM, 2).astype(f32) / HEAD_DIM)
    angles = frequency[:, None] * query_pos.astype(f32)[None, :]
    cosine, sine = jnp.cos(angles), jnp.sin(angles)
    gain_one, gain_two = gains[0].astype(f32), gains[1].astype(f32)

    if sharing > 1:
        sharers = [[g * sharing + i for i in range(sharing)] for g in range(F // sharing)]
        both = jnp.stack([w_key, w_value])
        both = lax.all_gather(both, "fsdp", axis=1, tiled=True, axis_index_groups=sharers)
        wk, wv = both[0], both[1]
    else:
        wk, wv = w_key, w_value
    w_qkv = jnp.concatenate([w_query, wk, wv], axis=0)

    def rope(values, sign):
        v = values.reshape(-1, 2, HALF_DIM, values.shape[1] // tokens, tokens)
        cb, sb = cosine[:, None, :], sign * sine[:, None, :]
        top, low = v[:, 0], v[:, 1]
        out = jnp.stack([top * cb - low * sb, low * cb + top * sb], axis=1)
        return out.reshape(values.shape)

    x_float = own_x.astype(f32)
    n1, q, kv, mixed, x_groups, inverses = [], [], [], [], [], []
    attn_parts = [None] * F
    for g, group in enumerate(attention_groups):
        x_group = joined([x_pieces[k] for k in group])
        if g == 0:
            x_group, w_out_rows = lax.optimization_barrier((x_group, w_out_rows))
            w_out = gather_rows(w_out_rows)
        inv_group = inverse_norm(x_group.astype(f32))
        n1_group = (x_group.astype(f32) * inv_group * gain_one).astype(bf16)
        x_groups.append(x_group)
        inverses.append(inv_group)
        lin = dot(w_qkv, n1_group, 1, 1)
        q_group = rope(lin[:q_rows], 1.0).astype(bf16) * jnp.asarray(score_scale, bf16)
        kv_own = jnp.concatenate(
            [
                rope(lin[q_rows : q_rows + HEAD_DIM], 1.0).astype(bf16),
                lin[q_rows + HEAD_DIM :].astype(bf16),
            ]
        )
        kv_group = ctx_gather(kv_own)
        if g == 0:
            down_blocks = swap_blocks(column_blocks(after(w_down, kv_own), C, F))
        mixed_group = attend_forward(q_group, kv_group, bias)
        part = dot(mixed_group, w_out, 0, 1)
        for i, k in enumerate(group):
            attn_parts[k] = part[i * tokens : (i + 1) * tokens]
        n1.append(n1_group)
        q.append(q_group)
        kv.append(kv_group)
        mixed.append(mixed_group)
    dy_late = after(own_dy, x_pieces[F // 2])
    dy_pieces = [dy_late]
    for k in range(1, F):
        dy_pieces.append(fetch(dy_late, k, F))
    w_dn = gather_rows(after(down_blocks, mixed[0]))
    hidden = x_float + scatter_sum(attn_parts, F)
    inv_two = inverse_norm(hidden)
    hat_two = hidden * inv_two
    own_n2 = (hat_two * gain_two).astype(bf16)

    n2_pieces = gather_pieces(own_n2, F)
    n2, dy, inner, d_gate, d_up = [], [], [], [], []
    dn2_parts = [None] * F
    out_parts = [None] * F
    for group in ffn_groups:
        n2_group = joined([n2_pieces[k] for k in group])
        dy_group = joined([dy_pieces[k] for k in group])
        gate = dot(n2_group, w_gate, 1, 1)
        up = dot(n2_group, w_up, 1, 1)
        d_inner = dot(dy_group, w_dn, 1, 0)
        sig = jax.nn.sigmoid(gate)
        act = gate * sig
        inner_group = (act * up).astype(bf16)
        d_gate_group = (d_inner * up * sig * (1.0 + gate * (1.0 - sig))).astype(bf16)
        d_up_group = (d_inner * act).astype(bf16)
        part = dot(d_gate_group, w_gate, 1, 0) + dot(d_up_group, w_up, 1, 0)
        out_part = dot(inner_group, w_dn, 1, 1)
        for i, k in enumerate(group):
            dn2_parts[k] = part[i * tokens : (i + 1) * tokens]
            out_parts[k] = out_part[i * tokens : (i + 1) * tokens].astype(bf16)
        n2.append(n2_group)
        dy.append(dy_group)
        inner.append(inner_group)
        d_gate.append(d_gate_group)
        d_up.append(d_up_group)
    n2, dy, inner, d_gate, d_up = (joined(v) for v in (n2, dy, inner, d_gate, d_up))
    d_n2 = scatter_sum(dn2_parts, F)

    part_down = row_shares(dot(dy, inner, 0, 0).astype(bf16), C, F)
    part_gate = dot(d_gate, n2, 0, 0).astype(bf16)
    part_up = dot(d_up, n2, 0, 0).astype(bf16)
    d_n2 = after(d_n2, part_down, part_gate, part_up)

    def reduced(value):
        return lax.psum_scatter(value, "ctx", scatter_dimension=1, tiled=True)

    part_down = lax.psum_scatter(part_down, "ctx", scatter_dimension=0, tiled=True)
    grad_gate = reduced(part_gate)
    grad_up = reduced(part_up)

    scaled = d_n2 * gain_two
    inner_mean = jnp.mean(scaled * hidden, axis=-1, keepdims=True)
    d_hidden = own_dy.astype(f32) + inv_two * scaled - hidden * inv_two**3 * inner_mean
    gain_two_grad = jnp.sum(d_n2 * hat_two, axis=0)
    branch_pieces = gather_pieces(d_hidden.astype(bf16), F)

    branch, grads, first = [], None, 0
    for group in backward_groups:
        branch_group = joined([branch_pieces[k] for k in group])
        d_mixed = dot(w_out, branch_group, 0, 1).astype(bf16)
        grads = attend_backward(q[0], kv[0], bias, d_mixed, cosine, sine, first, grads)
        first += len(group)
        branch.append(branch_group)
    d_q, d_kv = [grads[0]], [ctx_sum_back(grads[1])]
    d_qkv = []
    dn1_parts = [None] * F
    gain_one_grad = jnp.zeros((width,), f32)
    for g, group in enumerate(attention_groups):
        dkv_group = d_kv[g].astype(f32)
        if sharing > 1:
            dkv_group = lax.psum(dkv_group, "fsdp", axis_index_groups=sharers)
        d_k = rope(dkv_group[:HEAD_DIM], -1.0).astype(bf16)
        d_v = dkv_group[HEAD_DIM:].astype(bf16)
        if sharing > 1:
            first = (z % sharing) * kv_rows
            d_k = lax.dynamic_slice_in_dim(d_k, first, kv_rows)
            d_v = lax.dynamic_slice_in_dim(d_v, first, kv_rows)
            w_own = jnp.concatenate([w_query, w_key, w_value], axis=0)
        else:
            w_own = w_qkv
        d_qkv.append(jnp.concatenate([d_q[g], d_k, d_v], axis=0))
        part = dot(d_qkv[g], w_own, 0, 0).astype(bf16)
        hat = x_groups[g].astype(f32) * inverses[g]
        gain_one_grad = gain_one_grad + jnp.sum(part.astype(f32) * hat, axis=0)
        for i, k in enumerate(group):
            dn1_parts[k] = part[i * tokens : (i + 1) * tokens]
    d_n1 = scatter_sum(dn1_parts, F)

    layer = hidden + scatter_sum([after(p, branch_pieces[2]) for p in out_parts], F)
    layer_out = layer.astype(bf16).reshape(1, tokens, width)

    branch, mixed, n1, d_qkv = joined(branch), joined(mixed, 1), joined(n1), joined(d_qkv, 1)
    part_out = row_shares(dot(branch, mixed, 0, 1).astype(bf16), C, F)
    part_out = ctx_sum_exchange(part_out.reshape(C, width // C, -1))
    gain_parts = jnp.stack([gain_one_grad, gain_two_grad]).reshape(2, F, gain_width)
    gain_parts = gain_parts.transpose(1, 0, 2).reshape(F, 2 * gain_width)
    share = width // C // F
    (grad_down, grad_out), grad_gains = own_rows_of(
        [part_down.reshape(F, share, -1), part_out.reshape(F, share, -1)], gain_parts
    )
    grad_gains = grad_gains.reshape(2, gain_width)
    grad_down, grad_out = grad_down.astype(f32), grad_out.astype(f32)
    g_qkv = dot(n1, d_qkv, 0, 1).astype(bf16)
    g_qkv = ctx_sum_scatter(g_qkv.reshape(C, width // C, -1)).T.astype(f32)
    d_n1 = after(d_n1, grad_gains, grad_out, grad_down)
    grad_gate = after(grad_gate, d_n1).astype(f32)
    grad_up = after(grad_up, d_n1).astype(f32)

    inv_one = inverse_norm(x_float)
    scaled = d_n1 * gain_one
    inner_mean = jnp.mean(scaled * x_float, axis=-1, keepdims=True)
    grad_inputs = d_hidden + inv_one * scaled - x_float * inv_one**3 * inner_mean
    grad_inputs = grad_inputs.reshape(1, tokens, width)
    grad_query = g_qkv[:q_rows]
    grad_key = g_qkv[q_rows : q_rows + kv_rows]
    grad_value = g_qkv[q_rows + kv_rows :]
    return (
        layer_out,
        grad_inputs,
        grad_gains,
        grad_query,
        grad_key,
        grad_value,
        grad_out,
        grad_gate,
        grad_up,
        grad_down,
    )


def solution(mesh):
    rows = P("fsdp", None)
    tokens = P("fsdp", "ctx", None)
    grads = P("fsdp", "ctx")
    return jax.shard_map(
        per_device,
        mesh=mesh,
        in_specs=(tokens, P(), P(None, "fsdp"), rows, rows, rows, rows, rows, rows, rows, tokens),
        out_specs=(tokens, tokens, P(None, "fsdp")) + (grads,) * 7,
        check_vma=False,
    )
```

time: 809 us -> 596 us (0.74)
  blocking collectives: 127 us -> 0 us
  waiting for transfers between devices: 335 us -> 251 us
  starting transfers between devices: 142 us -> 106 us
  other arithmetic: 20.4 us -> 46.1 us
    unnamed x9 -> x5, waiting for transfers between devices: 96.6 us -> 0.08 us
    ppermute x0 -> x25, waiting for transfers between devices: none -> 84.8 us  [the longest x11 66.8 us: swap(): return lax.ppermute(value, 'ctx', [(i, i ^ mask) for i in range(size)])]
    psum x1 -> x0, blocking collectives: 54 us -> none  [per_device(): lax.psum(jnp.stack([gain_one_grad, gain_two_grad]), ('ctx', 'fsdp'))]
    ppermute x12 -> x9, starting transfers between devices: 65.9 us -> 12.8 us  [fetch(): lax.ppermute(value, 'fsdp', [((i + k) % size, i) for i in range(size)])]
    ppermute x0 -> x25, starting transfers between devices: none -> 50.1 us  [the longest x4 23.9 us: scatter_sum(): up = lax.ppermute(far, 'fsdp', [(0, 1), (1, 2)])]
    all_gather x1 -> x0, blocking collectives: 45.7 us -> none  [per_device(): gains = lax.all_gather(norm_gains, 'fsdp', axis=1, tiled=True)]
    reduce_scatter x4 -> x3, waiting for transfers between devices: 42 us -> 0.04 us  [the longest x2 0.02 us: reduced(): return lax.psum_scatter(value, 'ctx', scatter_dimension=1, tiled=True)]
    ppermute x12 -> x8, starting transfers between devices: 59.7 us -> 19.4 us  [give(): lax.ppermute(value, 'fsdp', [(i, (i + k) % size) for i in range(size)])]
  transfers between devices with their start and end apart: 36 -> 52, of which waited for: 17 -> 22; matrix products, arithmetic and copies ran while one was open for 13% -> 24% of each run, Pallas kernels for 2% -> 7%
where the time goes in v2:
time: 596 us; the launch traced here: 586 us
  waiting for transfers between devices  251 us (42%)
  starting transfers between devices  106 us (18%)
  matrix products  72.9 us (12%)
  local copies, waits for them, and re-layouts  53.5 us (9%)
  other arithmetic  46.1 us (8%)
  Pallas kernels  40.9 us (7%)
  between operations  15.4 us (3%)
    ppermute x9, waiting for transfers between devices, fetch(): lax.ppermute(value, 'fsdp', [((i + k) % size, i) for i in range(size)])  91.7 us
    dot_general x16, matrix products, dot(): lax.dot_general(a, b, (((ca,), (cb,)), ((), ())), preferred_element_type=...  72.9 us
    ppermute x11, waiting for transfers between devices, swap(): return lax.ppermute(value, 'ctx', [(i, i ^ mask) for i in range(size)])  66.8 us
    ppermute x8, waiting for transfers between devices, give(): lax.ppermute(value, 'fsdp', [(i, (i + k) % size) for i in range(size)])  55.2 us
    pallas_call x2, Pallas kernels, attend_backward(): pl.pallas_call(body, out_shape=(jax.ShapeDtypeStruct(q.shape, bf16), jax....  25.3 us
    ppermute x4, starting transfers between devices, scatter_sum(): up = lax.ppermute(far, 'fsdp', [(0, 1), (1, 2)])  23.9 us
    all_to_all x3, waiting for transfers between devices, swap_blocks(): lax.all_to_all(blocks, 'fsdp', split_axis=0, concat_axis=0, tiled=True)  19.7 us
    ppermute x8, starting transfers between devices, give(): lax.ppermute(value, 'fsdp', [(i, (i + k) % size) for i in range(size)])  19.4 us
  transfers between devices with their start and end apart: 52, of which 22 were waited for; matrix products, arithmetic and copies ran while one was open for 24% of the time, Pallas kernels for 7%

profile of v2, /device:TPU:0, one launch (start us, length us, event | category | flops | bytes accessed | tf_op | source)
XLA Modules:
  0.0 586.0 jit_solution(3200993430092960854)
XLA Ops:
  7.2 5.1 collective-permute-start
  20.1 4.9 collective-permute-done
  26.5 9.6 %collective-permute-done.1 = bf16[128,2048]{1,0:T(8,128)(2,1)} collective-permute-done((bf16[128,2048]{1,0:T(8,128)(2,1)}, bf16[128,2048]{1,0:T(8,128)(2,1)}, u32[]{:S(2)}, u32[]{:S(2)}) %collective-permute-start.1) | collective-permute-done | bytes 524320 | tf_op jit(solution)/shard_map/ppermute | solution.py:177
  37.7 4.7 all-to-all-start
  43.3 10.1 %all-to-all-done = bf16[4,66,512]{2,1,0:T(8,128)(2,1)S(1)} async-done(((bf16[4,66,512]{2,1,0:T(8,128)(2,1)}), bf16[4,66,512]{2,1,0:T(8,128)(2,1)S(1)}, u32[]{:S(2)}, u32[]{:S(2)}) %all-to-all-start) | async-done | bytes 270368 | tf_op jit(solution)/shard_map/all_to_all | solution.py:278
  53.4 6.7 %all-to-all-start.1 = ((bf16[4,64,1408]{2,1,0:T(8,128)(2,1)}), bf16[4,64,1408]{2,1,0:T(8,128)(2,1)S(1)}, u32[]{:S(2)}, u32[]{:S(2)}) async-start(bf16[4,64,1408]{2,1,0:T(8,128)(2,1)} %copy.53), calls=%async_computation.1 | async-start | bytes 1441792 | tf_op jit(solution)/shard_map/all_to_all | solution.py:278
  75.7 5.3 collective-permute-done.5
  87.0 15.6 %attend_forward.1 = bf16[512,512]{1,0:T(8,128)(2,1)} custom-call(bf16[512,512]{1,0:T(8,128)(2,1)} %bitcast.142, bf16[8,128,512]{2,1,0:T(8,128)(2,1)} %pad_maximum_fusion.4.kv_ref.refs_1_, f32[1024,128]{1,0:T(8,128)} %compare_select_fusion.bias_ref.refs_2_), custom_call_target="tpu_custom_call" | custom-call | flops 1073741824 | bytes 2097152 | tf_op jit(solution)/shard_map/attend_forward/pallas_call | solution.py:112
  106.8 4.1 collective-permute-start.7
  111.6 11.1 %collective-permute-done.7 = bf16[128,2048]{1,0:T(8,128)(2,1)S(1)} collective-permute-done((bf16[128,2048]{1,0:T(8,128)(2,1)S(1)}, bf16[128,2048]{1,0:T(8,128)(2,1)S(1)}, u32[]{:S(2)}, u32[]{:S(2)}) %collective-permute-start.7) | collective-permute-done | bytes 524320 | tf_op jit(solution)/shard_map/ppermute | solution.py:201
  123.0 3.7 collective-permute-start.10
  129.0 11.9 %collective-permute-done.10 = bf16[128,2048]{1,0:T(8,128)(2,1)S(1)} collective-permute-done((bf16[128,2048]{1,0:T(8,128)(2,1)S(1)}, bf16[128,2048]{1,0:T(8,128)(2,1)S(1)}, u32[]{:S(2)}, u32[]{:S(2)}) %collective-permute-start.10) | collective-permute-done | bytes 524320 | tf_op jit(solution)/shard_map/ppermute | solution.py:181
  140.9 11.1 %collective-permute-done.8 = bf16[128,2048]{1,0:T(8,128)(2,1)S(1)} collective-permute-done((bf16[128,2048]{1,0:T(8,128)(2,1)S(1)}, bf16[128,2048]{1,0:T(8,128)(2,1)S(1)}, u32[]{:S(2)}, u32[]{:S(2)}) %collective-permute-start.8) | collective-permute-done | bytes 524320 | tf_op jit(solution)/shard_map/ppermute | solution.py:181
  158.4 20.3 %collective-permute-done.11 = bf16[128,2048]{1,0:T(8,128)(2,1)S(1)} collective-permute-done((bf16[128,2048]{1,0:T(8,128)(2,1)S(1)}, bf16[128,2048]{1,0:T(8,128)(2,1)S(1)}, u32[]{:S(2)}, u32[]{:S(2)}) %collective-permute-start.11) | collective-permute-done | bytes 524320 | tf_op jit(solution)/shard_map/ppermute | solution.py:177
  180.8 22.6 %collective-permute-done.15 = bf16[128,2048]{1,0:T(8,128)(2,1)S(1)} collective-permute-done((bf16[128,2048]{1,0:T(8,128)(2,1)S(1)}, bf16[128,2048]{1,0:T(8,128)(2,1)S(1)}, u32[]{:S(2)}, u32[]{:S(2)}) %collective-permute-start.15) | collective-permute-done | bytes 524320 | tf_op jit(solution)/shard_map/ppermute | solution.py:177
  203.4 20.8 %collective-permute-done.17 = bf16[128,2048]{1,0:T(8,128)(2,1)S(1)} collective-permute-done((bf16[128,2048]{1,0:T(8,128)(2,1)S(1)}, bf16[128,2048]{1,0:T(8,128)(2,1)S(1)}, u32[]{:S(2)}, u32[]{:S(2)}) %collective-permute-start.17) | collective-permute-done | bytes 524320 | tf_op jit(solution)/shard_map/ppermute | solution.py:177
  225.8 5.1 fusion.49
  230.9 5.1 fusion.48
  242.7 5.5 multiply_convert_fusion
  248.2 3.7 convolution_convert_fusion.2
  255.5 7.6 %convolution_convert_fusion.1 = bf16[1408,2048]{1,0:T(8,128)(2,1)} fusion(bf16[512,1408]{1,0:T(8,128)(2,1)} %get-tuple-element.99, bf16[128,2048]{1,0:T(8,128)(2,1)} %copy-done.32, bf16[128,2048]{1,0:T(8,128)(2,1)} %copy-done.46, bf16[128,2048]{1,0:T(8,128)(2,1)} %copy-done.44, bf16[128,2048]{1,0:T(8,128)(2,1)} %copy-done.30), kind=kOutput, calls=%fused_computation.2 | convolution fusion | flops 2964062208 | bytes 9306112 | tf_op jit(solution)/shard_map/dot_general | solution.py:23
  263.2 6.0 %fusion.58 = f32[512,2048]{1,0:T(8,128)S(1)} fusion(bf16[512,1408]{1,0:T(8,128)(2,1)} %get-tuple-element.99, bf16[1408,2048]{1,0:T(8,128)(2,1)} %param.19), kind=kOutput, calls=%fused_computation.176 | convolution fusion | flops 2952790016 | bytes 11403264 | tf_op jit(solution)/shard_map/dot_general | solution.py:23
  269.2 5.9 %convolution_add_fusion = f32[512,2048]{1,0:T(8,128)S(1)} fusion(f32[512,2048]{1,0:T(8,128)S(1)} %fusion.58, bf16[512,1408]{1,0:T(8,128)(2,1)S(1)} %copy-done.49, bf16[1408,2048]{1,0:T(8,128)(2,1)} %param.20), kind=kOutput, calls=%fused_computation.12 | convolution fusion | flops 2953838592 | bytes 15597568 | tf_op jit(solution)/shard_map/dot_general | solution.py:23
  277.9 10.5 %collective-permute-start.18 = (bf16[128,2048]{1,0:T(8,128)(2,1)}, bf16[128,2048]{1,0:T(8,128)(2,1)}, u32[]{:S(2)}, u32[]{:S(2)}) collective-permute-start(bf16[128,2048]{1,0:T(8,128)(2,1)} %slice.326), channel_id=1, source_target_pairs={{0,1},{1,2},{4,5},{5,6},{8,9},{9,10},{12,13},{13,14},{16,17},{17,1... | collective-permute-start | bytes 1572872 | tf_op jit(solution)/shard_map/ppermute | solution.py:201
  289.9 6.8 %collective-permute-done.18 = bf16[128,2048]{1,0:T(8,128)(2,1)} collective-permute-done((bf16[128,2048]{1,0:T(8,128)(2,1)}, bf16[128,2048]{1,0:T(8,128)(2,1)}, u32[]{:S(2)}, u32[]{:S(2)}) %collective-permute-start.18) | collective-permute-done | bytes 524320 | tf_op jit(solution)/shard_map/ppermute | solution.py:201
  299.8 4.9 collective-permute-start.21
  306.6 5.0 convolution_convert_fusion
  311.6 7.7 %collective-permute-done.21 = bf16[128,2048]{1,0:T(8,128)(2,1)} collective-permute-done((bf16[128,2048]{1,0:T(8,128)(2,1)}, bf16[128,2048]{1,0:T(8,128)(2,1)}, u32[]{:S(2)}, u32[]{:S(2)}) %collective-permute-start.21) | collective-permute-done | bytes 524320 | tf_op jit(solution)/shard_map/ppermute | solution.py:181
  319.3 8.7 %collective-permute-done.19 = bf16[128,2048]{1,0:T(8,128)(2,1)} collective-permute-done((bf16[128,2048]{1,0:T(8,128)(2,1)}, bf16[128,2048]{1,0:T(8,128)(2,1)}, u32[]{:S(2)}, u32[]{:S(2)}) %collective-permute-start.19) | collective-permute-done | bytes 524320 | tf_op jit(solution)/shard_map/ppermute | solution.py:181
  333.8 8.1 %convolution_convert_fusion.6 = bf16[512,2048]{1,0:T(8,128)(2,1)} fusion(bf16[512,1408]{1,0:T(8,128)(2,1)S(1)} %copy-done.54, bf16[2048,1408]{1,0:T(8,128)(2,1)} %bitcast.129), kind=kOutput, calls=%fused_computation.15 | convolution fusion | flops 2953838592 | bytes 9306112 | tf_op jit(solution)/shard_map/dot_general | solution.py:23
  346.3 10.2 %collective-permute-done.24 = bf16[128,2048]{1,0:T(8,128)(2,1)} collective-permute-done((bf16[128,2048]{1,0:T(8,128)(2,1)S(1)}, bf16[128,2048]{1,0:T(8,128)(2,1)}, u32[]{:S(2)}, u32[]{:S(2)}) %collective-permute-start.24) | collective-permute-done | bytes 524320 | tf_op jit(solution)/shard_map/ppermute | solution.py:177
  361.3 18.0 %shard_map.195 = (bf16[512,512]{1,0:T(8,128)(2,1)}, bf16[8,128,512]{2,1,0:T(8,128)(2,1)}) custom-call(bf16[512,512]{1,0:T(8,128)(2,1)} %bitcast.143, bf16[8,128,512]{2,1,0:T(8,128)(2,1)} %pad_maximum_fusion.4.kv_ref.refs_1_, f32[1024,128]{1,0:T(8,128)} %compare_select_fusion.bias_ref.refs_2_, bf16[512,384]{1,0:T(8,128)(2,1)} %fusion.20.do_ref, ...), custom_call_target="tpu_custom_call" | custom-call | flops 2013265920 | bytes 2752512 | tf_op jit(solution)/shard_map/pallas_call | solution.py:159
  381.8 7.3 %shard_map.196 = (bf16[512,512]{1,0:T(8,128)(2,1)}, bf16[8,128,512]{2,1,0:T(8,128)(2,1)}) custom-call(bf16[512,512]{1,0:T(8,128)(2,1)} %bitcast.144, bf16[8,128,512]{2,1,0:T(8,128)(2,1)} %pad_maximum_fusion.4.kv_ref.refs_1_, f32[1024,128]{1,0:T(8,128)} %compare_select_fusion.bias_ref.refs_2_, ...), custom_call_target="tpu_custom_call", output_to_operand_aliasing={{0}: (6, {}), {1}: (7, {})} | custom-call | flops 671088640 | bytes 917504 | tf_op jit(solution)/shard_map/pallas_call | solution.py:159
  394.1 4.8 collective-permute-start.26
  403.1 3.7 all-to-all-start.2
  414.7 34.1 %collective-permute-done.31 = bf16[2,128,512]{2,1,0:T(8,128)(2,1)S(1)} collective-permute-done((bf16[2,128,512]{2,1,0:T(8,128)(2,1)S(1)}, bf16[2,128,512]{2,1,0:T(8,128)(2,1)S(1)}, u32[]{:S(2)}, u32[]{:S(2)}) %collective-permute-start.31) | collective-permute-done | bytes 262176 | tf_op jit(solution)/shard_map/ppermute | solution.py:212
  448.8 4.9 collective-permute-start.32
  458.2 5.2 fusion.3
  464.4 4.5 collective-permute-start.33
  470.4 3.6 convolution_convert_fusion.3
  474.0 3.5 constant_dynamic-slice_fusion.1
  494.2 4.3 all-to-all-start.3
  498.9 4.2 collective-permute-done.36
  503.1 11.4 %collective-permute-done.34 = bf16[128,2048]{1,0:T(8,128)(2,1)} collective-permute-done((bf16[128,2048]{1,0:T(8,128)(2,1)}, bf16[128,2048]{1,0:T(8,128)(2,1)}, u32[]{:S(2)}, u32[]{:S(2)}) %collective-permute-start.34) | collective-permute-done | bytes 524320 | tf_op jit(solution)/shard_map/ppermute | solution.py:181
  519.0 7.7 %collective-permute-done.38 = bf16[2,128,640]{1,2,0:T(8,128)(2,1)S(1)} collective-permute-done((bf16[2,128,640]{1,2,0:T(8,128)(2,1)S(1)}, bf16[2,128,640]{1,2,0:T(8,128)(2,1)S(1)}, u32[]{:S(2)}, u32[]{:S(2)}) %collective-permute-start.38) | collective-permute-done | bytes 327712 | tf_op jit(solution)/shard_map/ppermute | solution.py:212
  527.5 9.6 %all-to-all-done.3 = bf16[4,65,1920]{2,1,0:T(8,128)(2,1)} async-done(((bf16[4,65,1920]{2,1,0:T(8,128)(2,1)}), bf16[4,65,1920]{2,1,0:T(8,128)(2,1)}, u32[]{:S(2)}, u32[]{:S(2)}) %all-to-all-start.3) | async-done | bytes 998432 | tf_op jit(solution)/shard_map/all_to_all | solution.py:278
  542.0 3.6 all-to-all-start.4
  548.5 16.3 %collective-permute-done.39 = bf16[128,640]{0,1:T(8,128)(2,1)S(1)} collective-permute-done((bf16[128,640]{0,1:T(8,128)(2,1)S(1)}, bf16[128,640]{0,1:T(8,128)(2,1)S(1)}, u32[]{:S(2)}, u32[]{:S(2)}) %collective-permute-start.39) | collective-permute-done | bytes 163872 | tf_op jit(solution)/shard_map/ppermute | solution.py:212
  (336 shorter events, 155.4 us)
Async XLA Ops:
  7.2 17.8 %collective-permute-start = (bf16[128,2048]{1,0:T(8,128)(2,1)}, bf16[128,2048]{1,0:T(8,128)(2,1)}, u32[]{:S(2)}, u32[]{:S(2)}) collective-permute-start(bf16[128,2048]{1,0:T(8,128)(2,1)} %bitcast.125), channel_id=1, source_target_pairs={{1,0},{2,1},{3,2},{0,3},{5,4},{6,5},{7,6},{4,7},{9,8},{10,9},{11,1... | collective-permute-start | bytes 1572872 | tf_op jit(solution)/shard_map/ppermute | solution.py:177
  12.3 23.8 %collective-permute-start.1 = (bf16[128,2048]{1,0:T(8,128)(2,1)}, bf16[128,2048]{1,0:T(8,128)(2,1)}, u32[]{:S(2)}, u32[]{:S(2)}) collective-permute-start(bf16[128,2048]{1,0:T(8,128)(2,1)} %bitcast.126), channel_id=1, source_target_pairs={{3,0},{0,1},{1,2},{2,3},{7,4},{4,5},{5,6},{6,7},{11,8},{8,9},{9,10... | collective-permute-start | bytes 1572872 | tf_op jit(solution)/shard_map/ppermute | solution.py:177
  25.2 35.7 %collective-permute-start.2 = (bf16[128,2048]{1,0:T(8,128)(2,1)}, bf16[128,2048]{1,0:T(8,128)(2,1)S(1)}, u32[]{:S(2)}, u32[]{:S(2)}) collective-permute-start(bf16[128,2048]{1,0:T(8,128)(2,1)} %collective-permute-done), channel_id=1, source_target_pairs={{1,0},{2,1},{5,4},{6,5},{9,8},{10,9},{13,12},{14,13},{17,16},{18,1... | collective-permute-start | bytes 1572872 | tf_op jit(solution)/shard_map/ppermute | solution.py:189
  36.1 24.8 %collective-permute-start.3 = (bf16[128,2048]{1,0:T(8,128)(2,1)}, bf16[128,2048]{1,0:T(8,128)(2,1)S(1)}, u32[]{:S(2)}, u32[]{:S(2)}) collective-permute-start(bf16[128,2048]{1,0:T(8,128)(2,1)} %collective-permute-done.1), channel_id=1, source_target_pairs={{1,2},{2,3},{5,6},{6,7},{9,10},{10,11},{13,14},{14,15},{17,18},{18... | collective-permute-start | bytes 1572872 | tf_op jit(solution)/shard_map/ppermute | solution.py:190
  37.7 15.7 %all-to-all-start = ((bf16[4,66,512]{2,1,0:T(8,128)(2,1)}), bf16[4,66,512]{2,1,0:T(8,128)(2,1)S(1)}, u32[]{:S(2)}, u32[]{:S(2)}) async-start(bf16[4,66,512]{2,1,0:T(8,128)(2,1)} %copy.51), calls=%async_computation | async-start | bytes 589824 | tf_op jit(solution)/shard_map/all_to_all | solution.py:278
  53.4 49.2 %all-to-all-start.1 = ((bf16[4,64,1408]{2,1,0:T(8,128)(2,1)}), bf16[4,64,1408]{2,1,0:T(8,128)(2,1)S(1)}, u32[]{:S(2)}, u32[]{:S(2)}) async-start(bf16[4,64,1408]{2,1,0:T(8,128)(2,1)} %copy.53), calls=%async_computation.1 | async-start | bytes 1441792 | tf_op jit(solution)/shard_map/all_to_all | solution.py:278
  60.1 43.4 %all-gather.5.cloned.1.call-start = ((), (), s32[]{:S(2)}) async-start(), calls=%async_computation.11 | async-start | bytes 2359296 | tf_op jit(solution)/shard_map/all_gather | solution.py:283
  62.3 173.7 %all-gather.7.cloned.1.call-start = ((), (), s32[]{:S(2)}) async-start(), calls=%async_computation.12 | async-start | bytes 6488064 | tf_op jit(solution)/shard_map/all_gather | solution.py:283
  103.5 388.5 %reduce-scatter.4.cloned.1.call-start = ((), (), s32[]{:S(2)}) async-start(), calls=%async_computation.8 | async-start | bytes 6488064 | tf_op jit(solution)/shard_map/reduce_scatter | solution.py:485
  106.8 15.9 %collective-permute-start.7 = (bf16[128,2048]{1,0:T(8,128)(2,1)S(1)}, bf16[128,2048]{1,0:T(8,128)(2,1)S(1)}, u32[]{:S(2)}, u32[]{:S(2)}) collective-permute-start(bf16[128,2048]{1,0:T(8,128)(2,1)S(1)} %slice.327), channel_id=1, source_target_pairs={{0,1},{1,2},{4,5},{5,6},{8,9},{9,10},{12,13},{13,14},{16,17},{17,1... | collective-permute-start | bytes 1572872 | tf_op jit(solution)/shard_map/ppermute | solution.py:201
  110.9 11.8 %collective-permute-start.9 = (bf16[128,2048]{1,0:T(8,128)(2,1)S(1)}, bf16[128,2048]{1,0:T(8,128)(2,1)S(1)}, u32[]{:S(2)}, u32[]{:S(2)}) collective-permute-start(bf16[128,2048]{1,0:T(8,128)(2,1)S(1)} %slice.327), channel_id=1, source_target_pairs={{3,2},{2,1},{7,6},{6,5},{11,10},{10,9},{15,14},{14,13},{19,18},{18... | collective-permute-start | bytes 1572872 | tf_op jit(solution)/shard_map/ppermute | solution.py:202
  123.0 17.8 %collective-permute-start.10 = (bf16[128,2048]{1,0:T(8,128)(2,1)S(1)}, bf16[128,2048]{1,0:T(8,128)(2,1)S(1)}, u32[]{:S(2)}, u32[]{:S(2)}) collective-permute-start(bf16[128,2048]{1,0:T(8,128)(2,1)S(1)} %get-tuple-element.104), channel_id=1, source_target_pairs={{0,3},{1,0},{2,1},{3,2},{4,7},{5,4},{6,5},{7,6},{8,11},{9,8},{10,9... | collective-permute-start | bytes 1572872 | tf_op jit(solution)/shard_map/ppermute | solution.py:181
  126.8 25.3 %collective-permute-start.8 = (bf16[128,2048]{1,0:T(8,128)(2,1)S(1)}, bf16[128,2048]{1,0:T(8,128)(2,1)S(1)}, u32[]{:S(2)}, u32[]{:S(2)}) collective-permute-start(bf16[128,2048]{1,0:T(8,128)(2,1)S(1)} %get-tuple-element.103), channel_id=1, source_target_pairs={{0,1},{1,2},{2,3},{3,0},{4,5},{5,6},{6,7},{7,4},{8,9},{9,10},{10,1... | collective-permute-start | bytes 1572872 | tf_op jit(solution)/shard_map/ppermute | solution.py:181
  152.7 26.1 %collective-permute-start.11 = (bf16[128,2048]{1,0:T(8,128)(2,1)S(1)}, bf16[128,2048]{1,0:T(8,128)(2,1)S(1)}, u32[]{:S(2)}, u32[]{:S(2)}) collective-permute-start(bf16[128,2048]{1,0:T(8,128)(2,1)S(1)} %multiply_convert_fusion.3), channel_id=1, source_target_pairs={{1,0},{2,1},{3,2},{0,3},{5,4},{6,5},{7,6},{4,7},{9,8},{10,9},{11,1... | collective-permute-start | bytes 1572872 | tf_op jit(solution)/shard_map/ppermute | solution.py:177
  153.9 26.1 %collective-permute-start.12 = (bf16[128,2048]{1,0:T(8,128)(2,1)S(1)}, bf16[128,2048]{1,0:T(8,128)(2,1)S(1)}, u32[]{:S(2)}, u32[]{:S(2)}) collective-permute-start(bf16[128,2048]{1,0:T(8,128)(2,1)S(1)} %multiply_convert_fusion.3), channel_id=1, source_target_pairs={{3,0},{0,1},{1,2},{2,3},{7,4},{4,5},{5,6},{6,7},{11,8},{8,9},{9,10... | collective-permute-start | bytes 1572872 | tf_op jit(solution)/shard_map/ppermute | solution.py:177
  154.7 48.6 %collective-permute-start.15 = (bf16[128,2048]{1,0:T(8,128)(2,1)S(1)}, bf16[128,2048]{1,0:T(8,128)(2,1)S(1)}, u32[]{:S(2)}, u32[]{:S(2)}) collective-permute-start(bf16[128,2048]{1,0:T(8,128)(2,1)S(1)} %bitcast.135), channel_id=1, source_target_pairs={{1,0},{2,1},{3,2},{0,3},{5,4},{6,5},{7,6},{4,7},{9,8},{10,9},{11,1... | collective-permute-start | bytes 1572872 | tf_op jit(solution)/shard_map/ppermute | solution.py:177
  157.8 45.6 %collective-permute-start.16 = (bf16[128,2048]{1,0:T(8,128)(2,1)S(1)}, bf16[128,2048]{1,0:T(8,128)(2,1)S(1)}, u32[]{:S(2)}, u32[]{:S(2)}) collective-permute-start(bf16[128,2048]{1,0:T(8,128)(2,1)S(1)} %bitcast.136), channel_id=1, source_target_pairs={{3,0},{0,1},{1,2},{2,3},{7,4},{4,5},{5,6},{6,7},{11,8},{8,9},{9,10... | collective-permute-start | bytes 1572872 | tf_op jit(solution)/shard_map/ppermute | solution.py:177
  157.8 66.5 %collective-permute-start.17 = (bf16[128,2048]{1,0:T(8,128)(2,1)S(1)}, bf16[128,2048]{1,0:T(8,128)(2,1)S(1)}, u32[]{:S(2)}, u32[]{:S(2)}) collective-permute-start(bf16[128,2048]{1,0:T(8,128)(2,1)S(1)} %bitcast.137), channel_id=1, source_target_pairs={{2,0},{3,1},{0,2},{1,3},{6,4},{7,5},{4,6},{5,7},{10,8},{11,9},{8,1... | collective-permute-start | bytes 1572872 | tf_op jit(solution)/shard_map/ppermute | solution.py:177
  178.7 45.6 %collective-permute-start.13 = (bf16[128,2048]{1,0:T(8,128)(2,1)S(1)}, bf16[128,2048]{1,0:T(8,128)(2,1)S(1)}, u32[]{:S(2)}, u32[]{:S(2)}) collective-permute-start(bf16[128,2048]{1,0:T(8,128)(2,1)S(1)} %collective-permute-done.11), channel_id=1, source_target_pairs={{1,0},{2,1},{5,4},{6,5},{9,8},{10,9},{13,12},{14,13},{17,16},{18,1... | collective-permute-start | bytes 1572872 | tf_op jit(solution)/shard_map/ppermute | solution.py:189
  180.1 44.3 %collective-permute-start.14 = (bf16[128,2048]{1,0:T(8,128)(2,1)S(1)}, bf16[128,2048]{1,0:T(8,128)(2,1)S(1)}, u32[]{:S(2)}, u32[]{:S(2)}) collective-permute-start(bf16[128,2048]{1,0:T(8,128)(2,1)S(1)} %collective-permute-done.12), channel_id=1, source_target_pairs={{1,2},{2,3},{5,6},{6,7},{9,10},{10,11},{13,14},{14,15},{17,18},{18... | collective-permute-start | bytes 1572872 | tf_op jit(solution)/shard_map/ppermute | solution.py:190
  255.0 316.3 %reduce-scatter.6.cloned.1.call-start = ((), (), s32[]{:S(2)}) async-start(), calls=%async_computation.9 | async-start | bytes 6488064 | tf_op jit(solution)/shard_map/reduce_scatter | solution.py:483
  263.1 310.8 %reduce-scatter.8.cloned.1.call-start = ((), (), s32[]{:S(2)}) async-start(), calls=%async_computation.10 | async-start | bytes 6488064 | tf_op jit(solution)/shard_map/reduce_scatter | solution.py:483
  277.9 18.8 %collective-permute-start.18 = (bf16[128,2048]{1,0:T(8,128)(2,1)}, bf16[128,2048]{1,0:T(8,128)(2,1)}, u32[]{:S(2)}, u32[]{:S(2)}) collective-permute-start(bf16[128,2048]{1,0:T(8,128)(2,1)} %slice.326), channel_id=1, source_target_pairs={{0,1},{1,2},{4,5},{5,6},{8,9},{9,10},{12,13},{13,14},{16,17},{17,1... | collective-permute-start | bytes 1572872 | tf_op jit(solution)/shard_map/ppermute | solution.py:201
  299.8 19.5 %collective-permute-start.21 = (bf16[128,2048]{1,0:T(8,128)(2,1)}, bf16[128,2048]{1,0:T(8,128)(2,1)}, u32[]{:S(2)}, u32[]{:S(2)}) collective-permute-start(bf16[128,2048]{1,0:T(8,128)(2,1)} %get-tuple-element.102), channel_id=1, source_target_pairs={{0,3},{1,0},{2,1},{3,2},{4,7},{5,4},{6,5},{7,6},{8,11},{9,8},{10,9... | collective-permute-start | bytes 1572872 | tf_op jit(solution)/shard_map/ppermute | solution.py:181
  304.6 23.4 %collective-permute-start.19 = (bf16[128,2048]{1,0:T(8,128)(2,1)}, bf16[128,2048]{1,0:T(8,128)(2,1)}, u32[]{:S(2)}, u32[]{:S(2)}) collective-permute-start(bf16[128,2048]{1,0:T(8,128)(2,1)} %get-tuple-element.101), channel_id=1, source_target_pairs={{0,1},{1,2},{2,3},{3,0},{4,5},{5,6},{6,7},{7,4},{8,9},{9,10},{10,1... | collective-permute-start | bytes 1572872 | tf_op jit(solution)/shard_map/ppermute | solution.py:181
  331.7 13.3 %collective-permute-start.22 = (bf16[128,2048]{1,0:T(8,128)(2,1)S(1)}, bf16[128,2048]{1,0:T(8,128)(2,1)}, u32[]{:S(2)}, u32[]{:S(2)}) collective-permute-start(bf16[128,2048]{1,0:T(8,128)(2,1)S(1)} %get-tuple-element.90), channel_id=1, source_target_pairs={{1,0},{2,1},{3,2},{0,3},{5,4},{6,5},{7,6},{4,7},{9,8},{10,9},{11,1... | collective-permute-start | bytes 1572872 | tf_op jit(solution)/shard_map/ppermute | solution.py:177
  332.7 23.9 %collective-permute-start.24 = (bf16[128,2048]{1,0:T(8,128)(2,1)S(1)}, bf16[128,2048]{1,0:T(8,128)(2,1)}, u32[]{:S(2)}, u32[]{:S(2)}) collective-permute-start(bf16[128,2048]{1,0:T(8,128)(2,1)S(1)} %get-tuple-element.90), channel_id=1, source_target_pairs={{3,0},{0,1},{1,2},{2,3},{7,4},{4,5},{5,6},{6,7},{11,8},{8,9},{9,10... | collective-permute-start | bytes 1572872 | tf_op jit(solution)/shard_map/ppermute | solution.py:177
  345.0 34.3 %collective-permute-start.23 = (bf16[128,2048]{1,0:T(8,128)(2,1)}, bf16[128,2048]{1,0:T(8,128)(2,1)}, u32[]{:S(2)}, u32[]{:S(2)}) collective-permute-start(bf16[128,2048]{1,0:T(8,128)(2,1)} %collective-permute-done.22), channel_id=1, source_target_pairs={{1,0},{2,1},{5,4},{6,5},{9,8},{10,9},{13,12},{14,13},{17,16},{18,1... | collective-permute-start | bytes 1572872 | tf_op jit(solution)/shard_map/ppermute | solution.py:189
  356.6 22.7 %collective-permute-start.25 = (bf16[128,2048]{1,0:T(8,128)(2,1)}, bf16[128,2048]{1,0:T(8,128)(2,1)}, u32[]{:S(2)}, u32[]{:S(2)}) collective-permute-start(bf16[128,2048]{1,0:T(8,128)(2,1)} %collective-permute-done.24), channel_id=1, source_target_pairs={{1,2},{2,3},{5,6},{6,7},{9,10},{10,11},{13,14},{14,15},{17,18},{18... | collective-permute-start | bytes 1572872 | tf_op jit(solution)/shard_map/ppermute | solution.py:190
  391.1 15.7 %collective-permute-start.30 = (bf16[4,128,512]{2,1,0:T(8,128)(2,1)}, bf16[4,128,512]{2,1,0:T(8,128)(2,1)}, u32[]{:S(2)}, u32[]{:S(2)}) collective-permute-start(bf16[4,128,512]{2,1,0:T(8,128)(2,1)} %slice.198), channel_id=1, source_target_pairs={{0,4},{4,0},{8,12},{12,8},{16,20},{20,16},{24,28},{28,24},{1,5},{5... | collective-permute-start | bytes 1572872 | tf_op jit(solution)/shard_map/ppermute | solution.py:212
  392.5 17.8 %collective-permute-start.28 = (bf16[128,2048]{1,0:T(8,128)(2,1)}, bf16[128,2048]{1,0:T(8,128)(2,1)}, u32[]{:S(2)}, u32[]{:S(2)}) collective-permute-start(bf16[128,2048]{1,0:T(8,128)(2,1)} %get-tuple-element.37), channel_id=1, source_target_pairs={{3,2},{2,1},{7,6},{6,5},{11,10},{10,9},{15,14},{14,13},{19,18},{18... | collective-permute-start | bytes 1572872 | tf_op jit(solution)/shard_map/ppermute | solution.py:202
  394.1 59.6 %collective-permute-start.26 = (bf16[128,2048]{1,0:T(8,128)(2,1)}, bf16[128,2048]{1,0:T(8,128)(2,1)}, u32[]{:S(2)}, u32[]{:S(2)}) collective-permute-start(bf16[128,2048]{1,0:T(8,128)(2,1)} %get-tuple-element.37), channel_id=1, source_target_pairs={{0,1},{1,2},{4,5},{5,6},{8,9},{9,10},{12,13},{13,14},{16,17},{17,1... | collective-permute-start | bytes 1572872 | tf_op jit(solution)/shard_map/ppermute | solution.py:201
  403.1 86.5 %all-to-all-start.2 = ((bf16[8,256,512]{2,1,0:T(8,128)(2,1)}), bf16[8,256,512]{2,1,0:T(8,128)(2,1)S(1)}, u32[]{:S(2)}, u32[]{:S(2)}) async-start(bf16[8,256,512]{2,1,0:T(8,128)(2,1)} %bitcast.124), calls=%async_computation.3 | async-start | bytes 4194304 | tf_op jit(solution)/shard_map/all_to_all | solution.py:243
  408.3 40.5 %collective-permute-start.31 = (bf16[2,128,512]{2,1,0:T(8,128)(2,1)S(1)}, bf16[2,128,512]{2,1,0:T(8,128)(2,1)S(1)}, u32[]{:S(2)}, u32[]{:S(2)}) collective-permute-start(bf16[2,128,512]{2,1,0:T(8,128)(2,1)S(1)} %slice.251), channel_id=1, source_target_pairs={{0,16},{4,20},{8,24},{12,28},{16,0},{20,4},{24,8},{28,12},{1,17},{... | collective-permute-start | bytes 786440 | tf_op jit(solution)/shard_map/ppermute | solution.py:212
  412.2 70.1 %collective-permute-start.29 = (bf16[128,2048]{1,0:T(8,128)(2,1)}, bf16[128,2048]{1,0:T(8,128)(2,1)}, u32[]{:S(2)}, u32[]{:S(2)}) collective-permute-start(bf16[128,2048]{1,0:T(8,128)(2,1)} %add_convert_fusion.4), channel_id=1, source_target_pairs={{0,3},{1,0},{2,1},{3,2},{4,7},{5,4},{6,5},{7,6},{8,11},{9,8},{10,9... | collective-permute-start | bytes 1572872 | tf_op jit(solution)/shard_map/ppermute | solution.py:181
  448.8 9.1 %collective-permute-start.32 = (bf16[1,128,512]{2,1,0:T(8,128)(2,1)S(1)}, bf16[1,128,512]{2,1,0:T(8,128)(2,1)S(1)}, u32[]{:S(2)}, u32[]{:S(2)}) collective-permute-start(bf16[1,128,512]{2,1,0:T(8,128)(2,1)S(1)} %slice.253), channel_id=1, source_target_pairs={{0,8},{4,12},{8,0},{12,4},{16,24},{20,28},{24,16},{28,20},{1,9},{5... | collective-permute-start | bytes 393224 | tf_op jit(solution)/shard_map/ppermute | solution.py:212
  455.7 26.7 %collective-permute-start.27 = (bf16[128,2048]{1,0:T(8,128)(2,1)}, bf16[128,2048]{1,0:T(8,128)(2,1)}, u32[]{:S(2)}, u32[]{:S(2)}) collective-permute-start(bf16[128,2048]{1,0:T(8,128)(2,1)} %add_convert_fusion.5), channel_id=1, source_target_pairs={{0,1},{1,2},{2,3},{3,0},{4,5},{5,6},{6,7},{7,4},{8,9},{9,10},{10,1... | collective-permute-start | bytes 1572872 | tf_op jit(solution)/shard_map/ppermute | solution.py:181
  464.4 20.6 %collective-permute-start.33 = (bf16[128,2048]{1,0:T(8,128)(2,1)}, bf16[128,2048]{1,0:T(8,128)(2,1)}, u32[]{:S(2)}, u32[]{:S(2)}) collective-permute-start(bf16[128,2048]{1,0:T(8,128)(2,1)} %slice.260), channel_id=1, source_target_pairs={{0,1},{1,2},{4,5},{5,6},{8,9},{9,10},{12,13},{13,14},{16,17},{17,1... | collective-permute-start | bytes 1572872 | tf_op jit(solution)/shard_map/ppermute | solution.py:201
  468.9 16.1 %collective-permute-start.35 = (bf16[128,2048]{1,0:T(8,128)(2,1)}, bf16[128,2048]{1,0:T(8,128)(2,1)}, u32[]{:S(2)}, u32[]{:S(2)}) collective-permute-start(bf16[128,2048]{1,0:T(8,128)(2,1)} %slice.260), channel_id=1, source_target_pairs={{3,2},{2,1},{7,6},{6,5},{11,10},{10,9},{15,14},{14,13},{19,18},{18... | collective-permute-start | bytes 1572872 | tf_op jit(solution)/shard_map/ppermute | solution.py:202
  479.9 10.1 %collective-permute-start.37 = (bf16[2,2,256,640]{2,3,1,0:T(8,128)(2,1)}, bf16[2,2,256,640]{2,3,1,0:T(8,128)(2,1)}, u32[]{:S(2)}, u32[]{:S(2)}) collective-permute-start(bf16[2,2,256,640]{2,3,1,0:T(8,128)(2,1)} %bitcast.145), channel_id=1, source_target_pairs={{0,4},{4,0},{8,12},{12,8},{16,20},{20,16},{24,28},{28,24},{1,5},{5... | collective-permute-start | bytes 3932168 | tf_op jit(solution)/shard_map/ppermute | solution.py:212
  487.6 15.5 %collective-permute-start.36 = (bf16[128,2048]{1,0:T(8,128)(2,1)}, bf16[128,2048]{1,0:T(8,128)(2,1)}, u32[]{:S(2)}, u32[]{:S(2)}) collective-permute-start(bf16[128,2048]{1,0:T(8,128)(2,1)} %get-tuple-element.108), channel_id=1, source_target_pairs={{0,3},{1,0},{2,1},{3,2},{4,7},{5,4},{6,5},{7,6},{8,11},{9,8},{10,9... | collective-permute-start | bytes 1572872 | tf_op jit(solution)/shard_map/ppermute | solution.py:181
  487.6 27.0 %collective-permute-start.34 = (bf16[128,2048]{1,0:T(8,128)(2,1)}, bf16[128,2048]{1,0:T(8,128)(2,1)}, u32[]{:S(2)}, u32[]{:S(2)}) collective-permute-start(bf16[128,2048]{1,0:T(8,128)(2,1)} %get-tuple-element.107), channel_id=1, source_target_pairs={{0,1},{1,2},{2,3},{3,0},{4,5},{5,6},{6,7},{7,4},{8,9},{9,10},{10,1... | collective-permute-start | bytes 1572872 | tf_op jit(solution)/shard_map/ppermute | solution.py:181
  494.2 42.9 %all-to-all-start.3 = ((bf16[4,65,1920]{2,1,0:T(8,128)(2,1)}), bf16[4,65,1920]{2,1,0:T(8,128)(2,1)}, u32[]{:S(2)}, u32[]{:S(2)}) async-start(bf16[4,65,1920]{2,1,0:T(8,128)(2,1)} %pad_maximum_fusion.3), calls=%async_computation.4 | async-start | bytes 2211840 | tf_op jit(solution)/shard_map/all_to_all | solution.py:278
  498.8 19.2 %collective-permute-start.40 = (bf16[2,128,640]{1,2,0:T(8,128)(2,1)S(1)}, bf16[2,128,640]{1,2,0:T(8,128)(2,1)S(1)}, u32[]{:S(2)}, u32[]{:S(2)}) collective-permute-start(bf16[2,128,640]{1,2,0:T(8,128)(2,1)S(1)} %dynamic-slice_bitcast_fusion), channel_id=1, source_target_pairs={{0,16},{4,20},{8,24},{12,28},{16,0},{20,4},{24,8},{28,12},{1,17},{... | collective-permute-start | bytes 983048 | tf_op jit(solution)/shard_map/ppermute | solution.py:212
  516.2 10.6 %collective-permute-start.38 = (bf16[2,128,640]{1,2,0:T(8,128)(2,1)S(1)}, bf16[2,128,640]{1,2,0:T(8,128)(2,1)S(1)}, u32[]{:S(2)}, u32[]{:S(2)}) collective-permute-start(bf16[2,128,640]{1,2,0:T(8,128)(2,1)S(1)} %dynamic-slice_bitcast_fusion.1), channel_id=1, source_target_pairs={{0,8},{4,12},{8,0},{12,4},{16,24},{20,28},{24,16},{28,20},{1,9},{5... | collective-permute-start | bytes 983048 | tf_op jit(solution)/shard_map/ppermute | solution.py:212
  518.7 28.8 %collective-permute-start.41 = (bf16[128,640]{0,1:T(8,128)(2,1)}, bf16[128,640]{0,1:T(8,128)(2,1)}, u32[]{:S(2)}, u32[]{:S(2)}) collective-permute-start(bf16[128,640]{0,1:T(8,128)(2,1)} %dynamic-slice_bitcast_fusion.2), channel_id=1, source_target_pairs={{0,8},{4,12},{8,0},{12,4},{16,24},{20,28},{24,16},{28,20},{1,9},{5... | collective-permute-start | bytes 491528 | tf_op jit(solution)/shard_map/ppermute | solution.py:212
  542.0 24.4 %all-to-all-start.4 = ((bf16[8,66,960]{2,1,0:T(8,128)(2,1)}), bf16[8,66,960]{2,1,0:T(8,128)(2,1)S(1)}, u32[]{:S(2)}, u32[]{:S(2)}) async-start(bf16[8,66,960]{2,1,0:T(8,128)(2,1)} %pad_maximum_fusion.2), calls=%async_computation.5 | async-start | bytes 2359296 | tf_op jit(solution)/shard_map/all_to_all | solution.py:309
  545.6 19.2 %collective-permute-start.39 = (bf16[128,640]{0,1:T(8,128)(2,1)S(1)}, bf16[128,640]{0,1:T(8,128)(2,1)S(1)}, u32[]{:S(2)}, u32[]{:S(2)}) collective-permute-start(bf16[128,640]{0,1:T(8,128)(2,1)S(1)} %dynamic-slice_bitcast_fusion.3), channel_id=1, source_target_pairs={{0,16},{4,20},{8,24},{12,28},{16,0},{20,4},{24,8},{28,12},{1,17},{... | collective-permute-start | bytes 491528 | tf_op jit(solution)/shard_map/ppermute | solution.py:212
  (63 other events, 1059.5 us)
Sparse Core Ops, SparseCore 0:
  63.4 31.0 all-gather.4
  103.6 44.5 all-gather.6
  255.1 65.3 reduce-scatter.3
  323.8 58.8 reduce-scatter.5
  392.6 77.9 reduce-scatter.7
